TPU v7x, 256 devices: a whole 4x4x8 slice. The times are simulated.
256 devices in a mesh: rows: 64 (over z, x, core), heads: 4 (over y).
Axes of the slice: x: 4, y: 4, z: 8, core: 2. Of those that a mesh axis runs over, the one named last changes fastest.
Arguments:
- sheet: bfloat16 [1024, 256, 768], P('rows'), may hold values from -16 to 16
- w_query: bfloat16 [768, 768], P(None, 'heads'), may hold values from -0.21875 to 0.21875
- w_key: bfloat16 [768, 768], P(None, 'heads'), may hold values from -0.21875 to 0.21875
- w_value: bfloat16 [768, 768], P(None, 'heads'), may hold values from -0.21875 to 0.21875
- cotangent: bfloat16 [1024, 256, 768], P('rows', None, 'heads'), may hold values from -6 to 6
- lengths: int32 [1024], P('rows'), may hold values from 32 to 256
Outputs:
- input_grad: bfloat16 [1024, 256, 768], P('rows', None, 'heads')
- weight_grad: float32 [768, 3, 768], P('rows', None, 'heads')
All inputs are finite; a program needn't handle non-finite values.
Results may differ from a plain program's by a relative error of at most 0.013.
Values may be sent and summed in bfloat16 or wider, within the bound.
A program may use at most 128 MiB of HBM per device.

v0:
```python
import jax
import jax.numpy as jnp
from jax import lax
from jax.sharding import PartitionSpec as P

HEAD_DIM = 64


def softmax_back(logits, dprob, scale):
    probs = jax.nn.softmax(scale * logits, axis=-1)
    inner = jnp.sum(probs * dprob, axis=-1, keepdims=True)
    dscore = scale * probs * (dprob - inner)
    return (probs.astype(jnp.bfloat16), dscore.astype(jnp.bfloat16))


def body(sheet, w_query, w_key, w_value, cotangent, lengths):
    row_dev, cols, width = sheet.shape
    local = w_query.shape[1]
    heads_here = local // HEAD_DIM
    total_rows = row_dev * lax.axis_size("rows")
    scale = 1.0 / jnp.sqrt(jnp.float32(HEAD_DIM * total_rows))
    valid = (jnp.arange(cols, dtype=jnp.int32)[None, :] < lengths[:, None]).astype(jnp.float32)
    weights = jnp.concatenate([w_query, w_key, w_value], axis=1)
    flat = sheet.reshape(row_dev * cols, width)
    projected = jnp.dot(flat, weights, preferred_element_type=jnp.float32).reshape(
        row_dev, cols, 3 * local
    )
    projected = (projected * valid[..., None]).astype(jnp.bfloat16)
    split = (row_dev, cols, heads_here, HEAD_DIM)
    query = projected[..., :local].reshape(split)
    key = projected[..., local : 2 * local].reshape(split)
    value = projected[..., 2 * local :].reshape(split)
    grad_out = cotangent.reshape(split)
    logit_part = jnp.einsum("rihd,rjhd->hij", query, key, preferred_element_type=jnp.float32)
    dprob_part = jnp.einsum("rihd,rjhd->hij", grad_out, value, preferred_element_type=jnp.float32)
    logits, dprob = lax.psum((logit_part, dprob_part), "rows")
    probs_b, dscore = softmax_back(logits, dprob, scale)
    mask = valid[..., None]
    dquery = jnp.einsum("hij,rjhd->rihd", dscore, key, preferred_element_type=jnp.float32).reshape(
        row_dev, cols, local
    )
    dkey = jnp.einsum("hij,rihd->rjhd", dscore, query, preferred_element_type=jnp.float32).reshape(
        row_dev, cols, local
    )
    dvalue = jnp.einsum(
        "hij,rihd->rjhd", probs_b, grad_out, preferred_element_type=jnp.float32
    ).reshape(row_dev, cols, local)
    grads = (jnp.concatenate([dquery, dkey, dvalue], axis=-1) * mask).astype(jnp.bfloat16)
    flat_grads = grads.reshape(row_dev * cols, 3 * local)
    input_part = lax.dot_general(
        flat_grads, weights, (((1,), (1,)), ((), ())), preferred_element_type=jnp.float32
    )
    input_part = input_part.reshape(row_dev, cols, width).astype(jnp.bfloat16)
    input_grad = (
        lax.psum_scatter(input_part, "heads", scatter_dimension=2, tiled=True)
        .astype(jnp.float32)
        .astype(jnp.bfloat16)
    )
    rows_out = width // lax.axis_size("rows")
    weight_grad = lax.psum_scatter(
        lax.dot_general(
            flat, flat_grads, (((0,), (0,)), ((), ())), preferred_element_type=jnp.float32
        ),
        "rows",
        scatter_dimension=0,
        tiled=True,
    )
    return (input_grad, weight_grad.reshape(rows_out, 3, local))


def solution(mesh):
    in_specs = (
        P("rows", None, None),
        P(None, "heads"),
        P(None, "heads"),
        P(None, "heads"),
        P("rows", None, "heads"),
        P("rows"),
    )
    out_specs = (P("rows", None, "heads"), P("rows", None, "heads"))
    return jax.shard_map(body, mesh=mesh, in_specs=in_specs, out_specs=out_specs, check_vma=False)
```

profile of v0, /device:TPU:1, one launch (start us, length us, event | category | flops | bytes accessed | tf_op | source)
XLA Modules:
  0.0 515.0 jit_solution(13858921966701312197)
XLA Ops:
  7.2 0.0 all-reduce.7.cloned.1.call-start
  7.2 0.7 fusion.24
  7.9 1.0 constant_dynamic-update-slice_fusion.2
  8.9 1.0 constant_dynamic-update-slice_fusion.1
  9.9 1.0 constant_dynamic-update-slice_fusion
  10.9 0.0 copy-start.5
  10.9 6.3 %fusion.38 = f32[576,4096]{1,0:T(8,128)S(1)} fusion(bf16[768,576]{0,1:T(8,128)(2,1)S(1)} %constant_dynamic-update-slice_fusion, bf16[4096,768]{1,0:T(8,128)(2,1)} %bitcast.74), kind=kOutput, calls=%fused_computation.44 | convolution fusion | flops 3623878656 | bytes 16613376 | tf_op jit(solution)/shard_map/dot_general | solution.py:25
  17.2 0.0 copy-done.5
  17.2 1.1 fusion.2
  18.3 0.4 fusion.36
  18.7 0.0 copy-start.4
  18.7 0.0 copy-start
  18.7 1.1 copy-done.4
  19.8 1.6 convolution_bitcast_fusion.4
  21.4 0.0 copy-done
  21.4 1.6 convolution_bitcast_fusion.3
  23.0 0.0 all-reduce.7.cloned.1.call-update
  23.1 0.0 all-reduce.5.cloned.1.call-start
  23.1 1.2 copy.32
  24.4 189.9 %all-reduce.7.cloned.1.call-done = (f32[3,256,256]{2,1,0:T(8,128)}, f32[3,256,256]{2,1,0:T(8,128)}) async-done(((f32[3,256,256]{2,1,0:T(8,128)}, f32[3,256,256]{2,1,0:T(8,128)}), (f32[3,256,256]{2,1,0:T(8,128)}, f32[3,256,256]{2,1,0:T(8,128)})) %all-reduce.7.cloned.1.call-update) | async-done | bytes 1572880 | tf_op jit(solution)/shard_map/psum | solution.py:36
  214.3 1.5 fusion.37
  215.8 7.2 %convolution_bitcast_fusion.1 = f32[16,256,3,64]{1,3,0,2:T(8,128)} fusion(bf16[16,256,3,64]{1,3,2,0:T(8,128)(2,1)} %bitcast.71, f32[3,256,256]{2,1,0:T(8,128)} %get-tuple-element.9, f32[3,256,256]{2,1,0:T(8,128)S(1)} %get-tuple-element.14, f32[3,256]{1,0:T(4,128)S(1)} %get-tuple-element.13), kind=kOutput, calls=%fused_computation.8 | convolution fusion | flops 404030464 | bytes 6294528 | tf_op jit(solution)/shard_map/hij,rjhd->rihd/dot_general | solution.py:39
  223.0 6.8 %convolution_bitcast_fusion = f32[16,256,3,64]{1,3,0,2:T(8,128)} fusion(bf16[16,256,3,64]{1,3,2,0:T(8,128)(2,1)S(1)} %bitcast.69, f32[3,256,256]{2,1,0:T(8,128)} %get-tuple-element.9, f32[3,256,256]{2,1,0:T(8,128)S(1)} %get-tuple-element.14, f32[3,256]{1,0:T(4,128)S(1)} %get-tuple-element.13), kind=kOutput, calls=%fused_computation.7 | convolution fusion | flops 404030464 | bytes 6294528 | tf_op jit(solution)/shard_map/hij,rihd->rjhd/dot_general | solution.py:42
  229.8 0.0 copy-start.3
  229.8 2.3 copy.29
  232.1 0.6 copy-done.3
  232.6 2.1 copy.31
  234.7 5.0 fusion.19
  239.7 0.0 copy-start.1
  239.7 2.2 copy.33
  242.0 0.0 copy-start.2
  242.0 1.6 copy-done.2
  243.6 0.0 copy-done.1
  243.6 7.8 %convolution_bitcast_fusion.2 = f32[768,576]{0,1:T(8,128)} fusion(bf16[16,256,768]{2,1,0:T(8,128)(2,1)} %param.6, f32[16,256,192]{1,2,0:T(8,128)S(1)} %bitcast.65, f32[16,256,192]{1,2,0:T(8,128)S(1)} %bitcast.64, f32[16,256,192]{1,2,0:T(8,128)S(1)} %bitcast.61, f32[16,256]{1,0:T(8,128)S(1)} %fusion.24), kind=kOutput, calls=%fused_computation.11 | convolution fusion | flops 3633315840 | bytes 17514496 | tf_op jit(solution)/shard_map/dot_general | solution.py:61
  251.4 0.0 all-reduce.5.cloned.1.call-update
  251.5 0.2 reduce-scatter.3.cloned.1.call-start
  251.7 9.2 %convolution_convert_fusion = bf16[16,256,768]{1,2,0:T(8,128)(2,1)} fusion(bf16[768,576]{0,1:T(8,128)(2,1)} %copy-done.5, f32[16,256,192]{1,2,0:T(8,128)} %bitcast.66, f32[16,256,192]{1,2,0:T(8,128)} %bitcast.63, f32[16,256,192]{1,2,0:T(8,128)S(1)} %bitcast.62, f32[16,256]{1,0:T(8,128)S(1)} %fusion.24), kind=kOutput, calls=%fused_computation.6 | convolution fusion | flops 3636461568 | bytes 16629760 | tf_op jit(solution)/shard_map/dot_general | solution.py:50
  260.9 0.0 copy-start.6
  260.9 0.0 reduce-scatter.3.cloned.1.call-update
  261.0 0.6 copy-done.6
  261.6 0.6 dynamic-slice
  262.9 175.5 %all-reduce.5.cloned.1.call-done = f32[768,576]{0,1:T(8,128)} async-done(((f32[768,576]{0,1:T(8,128)}), f32[768,576]{0,1:T(8,128)}) %all-reduce.5.cloned.1.call-update) | async-done | bytes 1769488
  438.3 1.2 constant_dynamic-slice_fusion
  439.5 0.8 copy.34
  440.4 68.1 %reduce-scatter.3.cloned.1.call-done = bf16[16,256,192]{1,2,0:T(8,128)(2,1)} async-done(((bf16[16,256,768]{1,2,0:T(8,128)(2,1)}), bf16[16,256,192]{1,2,0:T(8,128)(2,1)}) %reduce-scatter.3.cloned.1.call-update) | async-done | bytes 1572880 | tf_op jit(solution)/shard_map/reduce_scatter | solution.py:55
Async XLA Ops:
  7.2 207.1 %all-reduce.7.cloned.1.call-start = ((), (), s32[]{:S(2)}) async-start(), calls=%async_computation.3 | async-start | bytes 3145728 | tf_op jit(solution)/shard_map/psum | solution.py:36
  10.9 6.3 %copy-start.5 = (bf16[768,576]{0,1:T(8,128)(2,1)}, bf16[768,576]{0,1:T(8,128)(2,1)S(1)}, u32[]{:S(2)}) copy-start(bf16[768,576]{0,1:T(8,128)(2,1)S(1)} %constant_dynamic-update-slice_fusion) | copy-start | bytes 2654212
  18.7 1.1 copy-start.4
  18.7 2.7 copy-start
  23.1 415.3 %all-reduce.5.cloned.1.call-start = ((), (), s32[]{:S(2)}) async-start(), calls=%async_computation.2 | async-start | bytes 3538944
  229.8 2.8 copy-start.3
  239.7 3.9 copy-start.1
  242.0 1.6 copy-start.2
  251.5 257.0 %reduce-scatter.3.cloned.1.call-start = ((), (), s32[]{:S(2)}) async-start(), calls=%async_computation.1 | async-start | bytes 7864320 | tf_op jit(solution)/shard_map/reduce_scatter | solution.py:55
  260.9 0.7 copy-start.6
Sparse Core Ops, SparseCore 0:
  23.2 191.0 all-reduce.6
  251.6 186.7 all-reduce.4
  441.5 66.9 reduce-scatter.2
where the time goes:
time: 515 us
  waiting for transfers between devices  434 us (84%)
  matrix products  45.6 us (9%)
  local copies, waits for them, and re-layouts  17.7 us (3%)
  between operations  14.5 us (3%)
    psum x1, waiting for transfers between devices, body(): logits, dprob = lax.psum((logit_part, dprob_part), 'rows')  190 us
    unnamed x4, waiting for transfers between devices  176 us
    reduce_scatter x1, waiting for transfers between devices, body(): lax.psum_scatter(input_part, 'heads', scatter_dimension=2, tiled=True)  68.1 us
  transfers between devices with their start and end apart: 3, of which 3 were waited for; matrix products, arithmetic and copies ran while one was open for 3% of the time, Pallas kernels for 0%

commit v1 on v0

v1 whole, which is shorter than its diff:
```python
import functools

import jax
import jax.numpy as jnp
from jax import lax
from jax.experimental import pallas as pl
from jax.experimental.pallas import tpu as pltpu
from jax.sharding import PartitionSpec as P

HEAD_DIM = 64
MESH = pl.DeviceIdType.MESH
NX, NZ, NY = 4, 8, 4
NH = 3
F32 = jnp.float32
BF16 = jnp.bfloat16


def nt(a, b):
    return lax.dot_general(a, b, (((1,), (1,)), ((), ())), preferred_element_type=F32)


def nn(a, b):
    return lax.dot_general(a, b, (((1,), (0,)), ((), ())), preferred_element_type=F32)


def tn(a, b):
    return lax.dot_general(a, b, (((0,), (0,)), ((), ())), preferred_element_type=F32)


def kernel(
    scale,
    sheet_h, wq, wk, wv, cot_h, lens, out_h, wg_out,
    sheet, cot, w_t, w_cat, vm, q_t, k_t, v_t, g_t,
    u, a_recv, a_sum, x_recv, x_sum, z_recv, full, gat, prob, dsc,
    d_t, part, r2, rl, fin, out_v,
    wg_acc, wg_n, wg_b, wa_recv, wx_recv, wx_sum, wz_recv,
    s_sheet, s_cot, s_out,
    sa, ra, sx, rx, sz, rz, sd, rd, sgz, rgz, sgx, rgx, sgc, rgc,
    s2, r2s, sdir, rdir, srl, rrl, swa, rwa, swx, rwx, swz, rwz,
):
    ri = lax.axis_index("rows")
    y = lax.axis_index("heads")
    core = lax.rem(ri, 2)
    x = lax.rem(ri // 2, NX)
    z = ri // (2 * NX)
    other = 1 - core
    partner = {"rows": (z * NX + x) * 2 + other}
    xs = [lax.rem(x + k, NX) for k in range(1, NX)]
    zs = [lax.rem(z + k, NZ) for k in range(1, NZ)]
    xpeer = [{"rows": (z * NX + xk) * 2 + core} for xk in xs]
    zpeer = [{"rows": (zk * NX + x) * 2 + core} for zk in zs]
    up, dn, opp = lax.rem(y + 1, NY), lax.rem(y + 3, NY), lax.rem(y + 2, NY)
    d_up, d_dn = {"heads": up}, {"heads": dn}

    def remote(src, dst, ss, rs, dev):
        return pltpu.make_async_remote_copy(
            src_ref=src, dst_ref=dst, send_sem=ss, recv_sem=rs, device_id=dev, device_id_type=MESH
        )

    for r in range(16):
        pltpu.make_async_copy(sheet_h.at[r], sheet.at[r], s_sheet.at[r]).start()
        pltpu.make_async_copy(cot_h.at[r], cot.at[r], s_cot.at[r]).start()

    barrier = pltpu.get_barrier_semaphore()
    peers = [partner, d_up, d_dn] + xpeer + zpeer
    for dev in peers:
        pl.semaphore_signal(barrier, inc=1, device_id=dev, device_id_type=MESH)

    w_t[0:192] = wq[...].T
    w_t[192:384] = wk[...].T
    w_t[384:576] = wv[...].T
    w_cat[...] = w_t[...].T

    def mask_row(r, _):
        vm[pl.ds(r, 1), :] = (
            lax.broadcasted_iota(jnp.int32, (1, 256), 1) < lens[r]
        ).astype(F32)
        return 0

    for r in range(16):
        mask_row(r, 0)

    def split_rows(ref, r, mat):
        at = pl.multiple_of(r * 64, 64)
        for h in range(NH):
            ref[h, pl.ds(at, 64), :] = mat[h * 64:(h + 1) * 64].astype(BF16)

    def value_row(r, _):
        pltpu.make_async_copy(sheet_h.at[r], sheet.at[r], s_sheet.at[r]).wait()
        pltpu.make_async_copy(cot_h.at[r], cot.at[r], s_cot.at[r]).wait()
        mat = nt(w_t[384:576], sheet[r]) * vm[pl.ds(r, 1), :]
        split_rows(v_t, r, mat)
        split_rows(g_t, r, cot[r].T)
        return 0

    lax.fori_loop(0, 16, value_row, 0)

    def core_copy(t, h):
        return remote(
            u.at[t, other, h], a_recv.at[t, h], sa.at[t, h], ra.at[t, h], partner
        )

    def x_copy(t, k):
        at = pl.multiple_of(xs[k] * 64, 64)
        return remote(
            a_sum.at[t, :, pl.ds(at, 64), :], x_recv.at[t, k], sx.at[t, k], rx.at[t, k], xpeer[k]
        )

    def z_copy(t, k):
        at = pl.multiple_of(zs[k] * 8, 8)
        return remote(
            x_sum.at[t, :, pl.ds(at, 8), :], z_recv.at[t, k], sz.at[t, k], rz.at[t, k], zpeer[k]
        )

    def outer(t, left, right):
        def one(h, _):
            mat = tn(left[h], right[h])
            u[t, 0, h] = mat[:, :128]
            u[t, 1, h] = mat[:, 128:]
            core_copy(t, h).start()
            return 0

        return one

    def add_core(t):
        for h in range(NH):
            core_copy(t, h).wait_recv()
            a_sum[t, h] = u[t, core, h] + a_recv[t, h]
        for k in range(NX - 1):
            x_copy(t, k).start()

    def add_x(t):
        for k in range(NX - 1):
            x_copy(t, k).wait_recv()
        mine = pl.multiple_of(x * 64, 64)
        x_sum[t] = a_sum[t, :, pl.ds(mine, 64), :] + x_recv[t, 0] + x_recv[t, 1] + x_recv[t, 2]
        for k in range(NZ - 1):
            z_copy(t, k).start()

    def add_z(t):
        for k in range(NZ - 1):
            z_copy(t, k).wait_recv()
        mine = pl.multiple_of(z * 8, 8)
        total = x_sum[t, :, pl.ds(mine, 8), :]
        for k in range(NZ - 1):
            total = total + z_recv[t, k]
        full[core, t] = total

    pl.semaphore_wait(barrier, len(peers))
    lax.fori_loop(0, NH, outer(0, g_t, v_t), 0)

    def query_rows(lo, hi):
        def one(r, _):
            mat = nt(w_t[0:384], sheet[r]) * vm[pl.ds(r, 1), :]
            split_rows(q_t, r, mat[:192])
            split_rows(k_t, r, mat[192:])
            return 0

        lax.fori_loop(lo, hi, one, 0)

    query_rows(0, 5)
    add_core(0)
    query_rows(5, 16)
    add_x(0)
    lax.fori_loop(0, NH, outer(1, q_t, k_t), 0)
    add_core(1)
    add_z(0)
    add_x(1)
    add_z(1)

    half_copy = remote(full.at[core], full.at[core], sd.at[0], rd.at[0], partner)
    half_copy.start()
    half_copy.wait_recv()

    dprob = jnp.concatenate([full[0, 0], full[1, 0]], axis=-1)
    logits = jnp.concatenate([full[0, 1], full[1, 1]], axis=-1) * scale
    top = jnp.max(logits, axis=-1, keepdims=True)
    ex = jnp.exp(logits - top)
    probs = ex / jnp.sum(ex, axis=-1, keepdims=True)
    inner = jnp.sum(probs * dprob, axis=-1, keepdims=True)
    dscore = scale * probs * (dprob - inner)
    tile = jnp.concatenate([probs, dscore], axis=1).astype(BF16)
    block = x * NZ + z
    gat[core, block] = jnp.where(core == 0, tile[:, :, :128].astype(F32), tile[:, :, 128:].astype(F32)).astype(BF16)

    gz = [
        remote(gat.at[core, block], gat.at[core, block], sgz.at[k], rgz.at[k], zpeer[k])
        for k in range(NZ - 1)
    ]
    for c in gz:
        c.start()
    for c in gz:
        c.wait_recv()

    def gx_copy(k):
        src = gat.at[core, pl.ds(pl.multiple_of(x * NZ, NZ), NZ)]
        return remote(src, src, sgx.at[k], rgx.at[k], xpeer[k])

    def gc_copy(k):
        owner = lax.rem(x + NX - k, NX)
        src = gat.at[core, pl.ds(pl.multiple_of(owner * NZ, NZ), NZ)]
        return remote(src, src, sgc.at[k], rgc.at[k], partner)

    for k in range(NX - 1):
        gx_copy(k).start()
    gc_copy(0).start()
    for k in range(NX - 1):
        gx_copy(k).wait_recv()
        gc_copy(k + 1).start()
    for k in range(NX):
        gc_copy(k).wait_recv()

    def unpack(h, _):
        for ch in range(2):
            mat = gat[ch, :, h].astype(F32)
            prob[h, :, ch * 128:(ch + 1) * 128] = mat[:, :8].reshape(256, 128).astype(BF16)
            dsc[h, :, ch * 128:(ch + 1) * 128] = mat[:, 8:].reshape(256, 128).astype(BF16)
        return 0

    lax.fori_loop(0, NH, unpack, 0)

    def back(h, _):
        at = pl.multiple_of(h * 64, 64)
        for t in range(3):
            if t == 0:
                mat = nt(k_t[h], dsc[h])
            elif t == 1:
                mat = nn(q_t[h], dsc[h])
            else:
                mat = nn(g_t[h], prob[h])
            for r in range(16):
                piece = (mat[r * 64:(r + 1) * 64] * vm[r:r + 1, :]).astype(BF16)
                lane = (r % 2) * 256
                d_t[r // 2, pl.ds(at + t * 192, 64), lane:lane + 256] = piece
        return 0

    lax.fori_loop(0, NH, back, 0)

    def rows_of(dest, lo, n):
        return pl.ds(pl.multiple_of(dest * 192 + lo, 16), n)

    def hop_up(c):
        return remote(part.at[c, rows_of(opp, 0, 96), :], r2.at[0, c], s2.at[0, c], r2s.at[0, c], d_up)

    def hop_dn(c):
        return remote(part.at[c, rows_of(opp, 96, 96), :], r2.at[1, c], s2.at[1, c], r2s.at[1, c], d_dn)

    def dir_up(c):
        return remote(
            part.at[c, rows_of(up, 96, 96), :], fin.at[0, c, 96:192, :], sdir.at[0, c], rdir.at[0, c], d_up
        )

    def dir_dn(c):
        return remote(
            part.at[c, rows_of(dn, 0, 96), :], fin.at[1, c, 0:96, :], sdir.at[1, c], rdir.at[1, c], d_dn
        )

    def rel_up(c):
        return remote(rl.at[0, c], fin.at[0, c, 0:96, :], srl.at[0, c], rrl.at[0, c], d_up)

    def rel_dn(c):
        return remote(rl.at[1, c], fin.at[1, c, 96:192, :], srl.at[1, c], rrl.at[1, c], d_dn)

    wg_acc[...] = jnp.zeros_like(wg_acc)

    def parts(c, _):
        part[c] = nn(w_cat[...], d_t[c]).astype(BF16)
        hop_up(c).start()
        hop_dn(c).start()
        dir_up(c).start()
        dir_dn(c).start()
        wg_acc[...] += nn(d_t[c], sheet[pl.ds(2 * c, 2)].reshape(512, 768))
        return 0

    lax.fori_loop(0, 8, parts, 0)

    def relay(c, _):
        hop_up(c).wait_recv()
        rl[0, c] = (part[c, rows_of(up, 0, 96), :].astype(F32) + r2[0, c].astype(F32)).astype(BF16)
        rel_up(c).start()
        hop_dn(c).wait_recv()
        rl[1, c] = (part[c, rows_of(dn, 96, 96), :].astype(F32) + r2[1, c].astype(F32)).astype(BF16)
        rel_dn(c).start()
        return 0

    wg_n[0:768] = wg_acc[...].T
    wg_n[768:784] = jnp.zeros((16, 576), F32)
    for g in range(64):
        gc, gx, gz_ = g % 2, (g // 2) % NX, g // (2 * NX)
        wg_b[gc, gx, gz_] = wg_n[12 * g:12 * g + 16, :]

    wa = remote(wg_b.at[other], wa_recv, swa.at[0], rwa.at[0], partner)
    wa.start()
    lax.fori_loop(0, 3, relay, 0)
    wa.wait_recv()
    wa_recv[...] = wa_recv[...] + wg_b[core]

    def wx_copy(k):
        return remote(wa_recv.at[xs[k]], wx_recv.at[k], swx.at[k], rwx.at[k], xpeer[k])

    def wz_copy(k):
        return remote(wx_sum.at[zs[k]], wz_recv.at[k], swz.at[k], rwz.at[k], zpeer[k])

    for k in range(NX - 1):
        wx_copy(k).start()
    lax.fori_loop(3, 6, relay, 0)
    for k in range(NX - 1):
        wx_copy(k).wait_recv()
    wx_sum[...] = wa_recv[x] + wx_recv[0] + wx_recv[1] + wx_recv[2]
    for k in range(NZ - 1):
        wz_copy(k).start()
    lax.fori_loop(6, 8, relay, 0)
    for k in range(NZ - 1):
        wz_copy(k).wait_recv()
    total = wx_sum[z]
    for k in range(NZ - 1):
        total = total + wz_recv[k]
    wg_out[...] = total[:12]

    def out_copy(c):
        return pltpu.make_async_copy(out_v.at[c], out_h.at[c], s_out.at[c])

    def finish(c, _):
        dir_up(c).wait_recv()
        dir_dn(c).wait_recv()
        rel_up(c).wait_recv()
        rel_dn(c).wait_recv()
        tot = part[c, rows_of(y, 0, 192), :].astype(F32) + fin[0, c].astype(F32) + fin[1, c].astype(F32)
        out_v[c] = tot.astype(BF16).T
        out_copy(c).start()
        return 0

    lax.fori_loop(0, 8, finish, 0)

    for t in range(2):
        for h in range(NH):
            core_copy(t, h).wait_send()
        for k in range(NX - 1):
            x_copy(t, k).wait_send()
        for k in range(NZ - 1):
            z_copy(t, k).wait_send()
    half_copy.wait_send()
    for c in gz:
        c.wait_send()
    for k in range(NX - 1):
        gx_copy(k).wait_send()
        wx_copy(k).wait_send()
    for k in range(NX):
        gc_copy(k).wait_send()
    wa.wait_send()
    for k in range(NZ - 1):
        wz_copy(k).wait_send()

    def drain(c, _):
        for cp in (hop_up, hop_dn, dir_up, dir_dn, rel_up, rel_dn):
            cp(c).wait_send()
        out_copy(c).wait()
        return 0

    lax.fori_loop(0, 8, drain, 0)


def body(sheet, w_query, w_key, w_value, cotangent, lengths):
    scale = float((HEAD_DIM * sheet.shape[0] * lax.axis_size("rows")) ** -0.5)
    vmem = pl.BlockSpec(memory_space=pltpu.VMEM)
    anyw = pl.BlockSpec(memory_space=pl.ANY)
    dma = pltpu.SemaphoreType.DMA
    V = pltpu.VMEM
    scratch = [
        V((16, 256, 768), BF16), V((16, 256, 192), BF16), V((576, 768), BF16), V((768, 576), BF16),
        V((16, 256), F32),
        V((3, 1024, 256), BF16), V((3, 1024, 256), BF16), V((3, 1024, 256), BF16), V((3, 1024, 256), BF16),
        V((2, 2, 3, 256, 128), F32), V((2, 3, 256, 128), F32), V((2, 3, 256, 128), F32),
        V((2, 3, 3, 64, 128), F32), V((2, 3, 64, 128), F32),
        V((2, 7, 3, 8, 128), F32), V((2, 2, 3, 8, 128), F32),
        V((2, 32, 3, 16, 128), BF16), V((3, 256, 256), BF16), V((3, 256, 256), BF16),
        V((8, 576, 512), BF16), V((8, 768, 512), BF16), V((2, 8, 96, 512), BF16), V((2, 8, 96, 512), BF16),
        V((2, 8, 192, 512), BF16), V((8, 512, 192), BF16),
        V((576, 768), F32), V((784, 576), F32), V((2, 4, 8, 16, 576), F32), V((4, 8, 16, 576), F32),
        V((3, 8, 16, 576), F32), V((8, 16, 576), F32), V((7, 16, 576), F32),
        dma((16,)), dma((16,)), dma((8,)),
        dma((2, 3)), dma((2, 3)), dma((2, 3)), dma((2, 3)), dma((2, 7)), dma((2, 7)), dma((1,)), dma((1,)),
        dma((7,)), dma((7,)), dma((3,)), dma((3,)), dma((4,)), dma((4,)),
        dma((2, 8)), dma((2, 8)), dma((2, 8)), dma((2, 8)), dma((2, 8)), dma((2, 8)),
        dma((1,)), dma((1,)), dma((3,)), dma((3,)), dma((7,)), dma((7,)),
    ]
    out, wg = pl.pallas_call(
        functools.partial(kernel, scale),
        out_shape=(jax.ShapeDtypeStruct((8, 512, 192), BF16), jax.ShapeDtypeStruct((12, 576), F32)),
        in_specs=[anyw, vmem, vmem, vmem, anyw, pl.BlockSpec(memory_space=pltpu.SMEM)],
        out_specs=(anyw, vmem),
        scratch_shapes=scratch,
        compiler_params=pltpu.CompilerParams(
            collective_id=0, has_side_effects=True, vmem_limit_bytes=63 * 1024 * 1024
        ),
    )(sheet, w_query, w_key, w_value, cotangent, lengths)
    return out.reshape(16, 256, 192), wg.reshape(12, 3, 192)


def solution(mesh):
    in_specs = (
        P("rows", None, None),
        P(None, "heads"),
        P(None, "heads"),
        P(None, "heads"),
        P("rows", None, "heads"),
        P("rows"),
    )
    out_specs = (P("rows", None, "heads"), P("rows", None, "heads"))
    return jax.shard_map(body, mesh=mesh, in_specs=in_specs, out_specs=out_specs, check_vma=False)
```

time: 515 us -> 125 us (0.24)
  waiting for transfers between devices: 434 us -> 0 us
  Pallas kernels: 0 us -> 111 us
  matrix products: 45.6 us -> 0 us
  between operations: 14.5 us -> 0.66 us
    psum x1 -> x0, waiting for transfers between devices: 190 us -> none  [body(): logits, dprob = lax.psum((logit_part, dprob_part), 'rows')]
    unnamed x4 -> x0, waiting for transfers between devices: 176 us -> none
    pallas_call x0 -> x1, Pallas kernels: none -> 111 us  [body(): pl.pallas_call(functools.partial(kernel, scale), out_shape=(jax.ShapeDtyp...]
    reduce_scatter x1 -> x0, waiting for transfers between devices: 68.1 us -> none  [body(): lax.psum_scatter(input_part, 'heads', scatter_dimension=2, tiled=True)]
    dot_general x7 -> x0, matrix products: 40.6 us -> none  [the longest x1 9.24 us: body(): lax.dot_general(flat_grads, weights, (((1,), (1,)), ((), ())), preferred_...]
    transpose x3 -> x0, local copies, waits for them, and re-layouts: 6.58 us -> none  [the longest x1 2.27 us: body(): jnp.einsum('hij,rjhd->rihd', dscore, key, preferred_element_type=jnp.floa...]
    unnamed x19 -> x9, local copies, waits for them, and re-layouts: 8.51 us -> 12.2 us
  transfers between devices with their start and end apart: 3 -> 0, of which waited for: 3 -> 0; matrix products, arithmetic and copies ran while one was open for 3% -> 0% of each run, Pallas kernels for 0% -> 0%
where the time goes in v1:
time: 125 us
  Pallas kernels  111 us (89%)
  local copies, waits for them, and re-layouts  12.9 us (10%)
    pallas_call x1, Pallas kernels, body(): pl.pallas_call(functools.partial(kernel, scale), out_shape=(jax.ShapeDtyp...  111 us
    unnamed x9, local copies, waits for them, and re-layouts  12.2 us

profile of v1, /device:TPU:1, one launch (start us, length us, event | category | flops | bytes accessed | tf_op | source)
XLA Modules:
  0.0 124.9 jit_solution(18420563784587936428)
XLA Ops:
  0.6 0.0 copy-start
  0.6 2.0 %copy.8.wq = bf16[768,192]{1,0:T(8,128)(2,1)} copy(bf16[768,192]{0,1:T(8,128)(2,1)} %param.7) | data formatting | bytes 589824 | tf_op args[1]
  2.6 1.9 %copy.9.wk = bf16[768,192]{1,0:T(8,128)(2,1)} copy(bf16[768,192]{0,1:T(8,128)(2,1)} %param.8) | data formatting | bytes 589824 | tf_op args[2]
  4.5 1.9 %copy.10.wv = bf16[768,192]{1,0:T(8,128)(2,1)} copy(bf16[768,192]{0,1:T(8,128)(2,1)} %param.9) | data formatting | bytes 589824 | tf_op args[3]
  6.4 0.0 copy-done
  6.4 2.5 %copy.11.cot_h = bf16[16,256,192]{2,1,0:T(8,128)(2,1)} copy(bf16[16,256,192]{1,2,0:T(8,128)(2,1)S(1)} %copy-done) | data formatting | bytes 3145728 | tf_op args[4]
  8.9 111.4 %shard_map.77 = (bf16[8,512,192]{2,1,0:T(8,128)(2,1)}, f32[12,576]{1,0:T(8,128)}) custom-call(bf16[16,256,768]{2,1,0:T(8,128)(2,1)} %sheet_h.1, bf16[768,192]{1,0:T(8,128)(2,1)} %copy.8.wq, bf16[768,192]{1,0:T(8,128)(2,1)} %copy.9.wk, bf16[768,192]{1,0:T(8,128)(2,1)} %copy.10.wv, bf16[16,256,192]{2,1,0:T(8,128)(2,1)} %copy.11.cot_h, s32[16]{0:T(128)} %lens.1), custom_call_target="tpu_custom_call" | custom-call | tf_op jit(solution)/shard_map/pallas_call | solution.py:387
  120.3 0.0 copy-start.1
  120.3 3.9 %copy.12 = bf16[16,256,192]{1,2,0:T(8,128)(2,1)} copy(bf16[16,256,192]{2,1,0:T(8,128)(2,1)} %bitcast.1) | data formatting | bytes 3145728
  124.2 0.0 copy-done.1
  124.2 0.7 reshape.11
Async XLA Ops:
  0.6 5.8 %copy-start = (bf16[16,256,192]{1,2,0:T(8,128)(2,1)S(1)}, bf16[16,256,192]{1,2,0:T(8,128)(2,1)}, u32[]{:S(2)}) copy-start(bf16[16,256,192]{1,2,0:T(8,128)(2,1)} %param.10) | copy-start | bytes 4718596
  120.3 3.9 %copy-start.1 = (f32[12,576]{1,0:T(8,128)S(1)}, f32[12,576]{1,0:T(8,128)}, u32[]{:S(2)}) copy-start(f32[12,576]{1,0:T(8,128)} %get-tuple-element.5) | copy-start | bytes 82948

commit v2 on v1

--- a/solution.py
+++ b/solution.py
@@ -30,11 +30,11 @@
 def kernel(
     scale,
     sheet_h, wq, wk, wv, cot_h, lens, out_h, wg_out,
-    sheet, cot, w_t, w_cat, vm, q_t, k_t, v_t, g_t,
+    sheet, w_t, w_cat, vm, q_t, k_t, v_t, g_t,
     u, a_recv, a_sum, x_recv, x_sum, z_recv, full, gat, prob, dsc,
     d_t, part, r2, rl, fin, out_v,
     wg_acc, wg_n, wg_b, wa_recv, wx_recv, wx_sum, wz_recv,
-    s_sheet, s_cot, s_out,
+    s_sheet, s_cot, s_w, s_out,
     sa, ra, sx, rx, sz, rz, sd, rd, sgz, rgz, sgx, rgx, sgc, rgc,
     s2, r2s, sdir, rdir, srl, rrl, swa, rwa, swx, rwx, swz, rwz,
 ):
@@ -57,43 +57,47 @@
             src_ref=src, dst_ref=dst, send_sem=ss, recv_sem=rs, device_id=dev, device_id_type=MESH
         )
 
+    def w_copy(t):
+        return pltpu.make_async_copy((wq, wk, wv)[t], w_t.at[192 * t:192 * t + 192], s_w.at[t])
+
+    def sheet_copy(r):
+        return pltpu.make_async_copy(sheet_h.at[r], sheet.at[r], s_sheet.at[r])
+
+    def cot_copy(r):
+        at = pl.multiple_of(r * 64, 64)
+        return pltpu.make_async_copy(cot_h.at[r], g_t.at[:, pl.ds(at, 64), :], s_cot.at[r])
+
+    w_copy(2).start()
     for r in range(16):
-        pltpu.make_async_copy(sheet_h.at[r], sheet.at[r], s_sheet.at[r]).start()
-        pltpu.make_async_copy(cot_h.at[r], cot.at[r], s_cot.at[r]).start()
+        sheet_copy(r).start()
+    for r in range(16):
+        cot_copy(r).start()
+    w_copy(0).start()
+    w_copy(1).start()
 
     barrier = pltpu.get_barrier_semaphore()
     peers = [partner, d_up, d_dn] + xpeer + zpeer
     for dev in peers:
         pl.semaphore_signal(barrier, inc=1, device_id=dev, device_id_type=MESH)
 
-    w_t[0:192] = wq[...].T
-    w_t[192:384] = wk[...].T
-    w_t[384:576] = wv[...].T
-    w_cat[...] = w_t[...].T
-
-    def mask_row(r, _):
-        vm[pl.ds(r, 1), :] = (
-            lax.broadcasted_iota(jnp.int32, (1, 256), 1) < lens[r]
-        ).astype(F32)
-        return 0
-
     for r in range(16):
-        mask_row(r, 0)
+        vm[r:r + 1, :] = (lax.broadcasted_iota(jnp.int32, (1, 256), 1) < lens[r]).astype(F32)
 
     def split_rows(ref, r, mat):
         at = pl.multiple_of(r * 64, 64)
         for h in range(NH):
             ref[h, pl.ds(at, 64), :] = mat[h * 64:(h + 1) * 64].astype(BF16)
 
-    def value_row(r, _):
-        pltpu.make_async_copy(sheet_h.at[r], sheet.at[r], s_sheet.at[r]).wait()
-        pltpu.make_async_copy(cot_h.at[r], cot.at[r], s_cot.at[r]).wait()
-        mat = nt(w_t[384:576], sheet[r]) * vm[pl.ds(r, 1), :]
-        split_rows(v_t, r, mat)
-        split_rows(g_t, r, cot[r].T)
-        return 0
-
-    lax.fori_loop(0, 16, value_row, 0)
+    def value_rows(i, _):
+        for n in range(4):
+            sheet_copy(4 * i + n).wait()
+        mat = nt(w_t[384:576], sheet[pl.ds(4 * i, 4)].reshape(1024, 768))
+        for n in range(4):
+            split_rows(v_t, 4 * i + n, mat[:, 256 * n:256 * n + 256] * vm[pl.ds(4 * i + n, 1), :])
+        return 0
+
+    w_copy(2).wait()
+    lax.fori_loop(0, 4, value_rows, 0)
 
     def core_copy(t, h):
         return remote(
@@ -146,21 +150,27 @@
             total = total + z_recv[t, k]
         full[core, t] = total
 
+    for r in range(16):
+        cot_copy(r).wait()
     pl.semaphore_wait(barrier, len(peers))
     lax.fori_loop(0, NH, outer(0, g_t, v_t), 0)
 
     def query_rows(lo, hi):
-        def one(r, _):
-            mat = nt(w_t[0:384], sheet[r]) * vm[pl.ds(r, 1), :]
-            split_rows(q_t, r, mat[:192])
-            split_rows(k_t, r, mat[192:])
+        def one(i, _):
+            mat = nt(w_t[0:384], sheet[pl.ds(4 * i, 4)].reshape(1024, 768))
+            for n in range(4):
+                sub = mat[:, 256 * n:256 * n + 256] * vm[pl.ds(4 * i + n, 1), :]
+                split_rows(q_t, 4 * i + n, sub[:192])
+                split_rows(k_t, 4 * i + n, sub[192:])
             return 0
 
         lax.fori_loop(lo, hi, one, 0)
 
-    query_rows(0, 5)
+    w_copy(0).wait()
+    w_copy(1).wait()
+    query_rows(0, 1)
     add_core(0)
-    query_rows(5, 16)
+    query_rows(1, 4)
     add_x(0)
     lax.fori_loop(0, NH, outer(1, q_t, k_t), 0)
     add_core(1)
@@ -170,6 +180,7 @@
 
     half_copy = remote(full.at[core], full.at[core], sd.at[0], rd.at[0], partner)
     half_copy.start()
+    w_cat[...] = w_t[...].T
     half_copy.wait_recv()
 
     dprob = jnp.concatenate([full[0, 0], full[1, 0]], axis=-1)
@@ -315,10 +326,12 @@
     total = wx_sum[z]
     for k in range(NZ - 1):
         total = total + wz_recv[k]
-    wg_out[...] = total[:12]
+    for t in range(3):
+        wg_out[:, t, :] = total[:12, 192 * t:192 * t + 192]
 
     def out_copy(c):
-        return pltpu.make_async_copy(out_v.at[c], out_h.at[c], s_out.at[c])
+        rows = pl.ds(2 * c, 2)
+        return pltpu.make_async_copy(out_v.at[rows], out_h.at[rows], s_out.at[c])
 
     def finish(c, _):
         dir_up(c).wait_recv()
@@ -326,7 +339,8 @@
         rel_up(c).wait_recv()
         rel_dn(c).wait_recv()
         tot = part[c, rows_of(y, 0, 192), :].astype(F32) + fin[0, c].astype(F32) + fin[1, c].astype(F32)
-        out_v[c] = tot.astype(BF16).T
+        out_v[2 * c] = tot[:, :256].astype(BF16)
+        out_v[2 * c + 1] = tot[:, 256:].astype(BF16)
         out_copy(c).start()
         return 0
 
@@ -367,7 +381,7 @@
     dma = pltpu.SemaphoreType.DMA
     V = pltpu.VMEM
     scratch = [
-        V((16, 256, 768), BF16), V((16, 256, 192), BF16), V((576, 768), BF16), V((768, 576), BF16),
+        V((16, 256, 768), BF16), V((576, 768), BF16), V((768, 576), BF16),
         V((16, 256), F32),
         V((3, 1024, 256), BF16), V((3, 1024, 256), BF16), V((3, 1024, 256), BF16), V((3, 1024, 256), BF16),
         V((2, 2, 3, 256, 128), F32), V((2, 3, 256, 128), F32), V((2, 3, 256, 128), F32),
@@ -375,10 +389,10 @@
         V((2, 7, 3, 8, 128), F32), V((2, 2, 3, 8, 128), F32),
         V((2, 32, 3, 16, 128), BF16), V((3, 256, 256), BF16), V((3, 256, 256), BF16),
         V((8, 576, 512), BF16), V((8, 768, 512), BF16), V((2, 8, 96, 512), BF16), V((2, 8, 96, 512), BF16),
-        V((2, 8, 192, 512), BF16), V((8, 512, 192), BF16),
+        V((2, 8, 192, 512), BF16), V((16, 192, 256), BF16),
         V((576, 768), F32), V((784, 576), F32), V((2, 4, 8, 16, 576), F32), V((4, 8, 16, 576), F32),
         V((3, 8, 16, 576), F32), V((8, 16, 576), F32), V((7, 16, 576), F32),
-        dma((16,)), dma((16,)), dma((8,)),
+        dma((16,)), dma((16,)), dma((3,)), dma((8,)),
         dma((2, 3)), dma((2, 3)), dma((2, 3)), dma((2, 3)), dma((2, 7)), dma((2, 7)), dma((1,)), dma((1,)),
         dma((7,)), dma((7,)), dma((3,)), dma((3,)), dma((4,)), dma((4,)),
         dma((2, 8)), dma((2, 8)), dma((2, 8)), dma((2, 8)), dma((2, 8)), dma((2, 8)),
@@ -386,15 +400,18 @@
     ]
     out, wg = pl.pallas_call(
         functools.partial(kernel, scale),
-        out_shape=(jax.ShapeDtypeStruct((8, 512, 192), BF16), jax.ShapeDtypeStruct((12, 576), F32)),
-        in_specs=[anyw, vmem, vmem, vmem, anyw, pl.BlockSpec(memory_space=pltpu.SMEM)],
+        out_shape=(jax.ShapeDtypeStruct((16, 192, 256), BF16), jax.ShapeDtypeStruct((12, 3, 192), F32)),
+        in_specs=[anyw] * 5 + [pl.BlockSpec(memory_space=pltpu.SMEM)],
         out_specs=(anyw, vmem),
         scratch_shapes=scratch,
         compiler_params=pltpu.CompilerParams(
-            collective_id=0, has_side_effects=True, vmem_limit_bytes=63 * 1024 * 1024
+            collective_id=0, has_side_effects=True, vmem_limit_bytes=56 * 1024 * 1024
         ),
-    )(sheet, w_query, w_key, w_value, cotangent, lengths)
-    return out.reshape(16, 256, 192), wg.reshape(12, 3, 192)
+    )(
+        sheet, w_query.T, w_key.T, w_value.T,
+        cotangent.transpose(0, 2, 1).reshape(16, NH, HEAD_DIM, 256), lengths,
+    )
+    return out.transpose(0, 2, 1), wg
 
 
 def solution(mesh):

time: 125 us -> 115 us (0.920)
  local copies, waits for them, and re-layouts: 12.9 us -> 3.33 us
    unnamed x9 -> x4, local copies, waits for them, and re-layouts: 12.2 us -> 3.33 us
where the time goes in v2:
time: 115 us
  Pallas kernels  111 us (97%)
  local copies, waits for them, and re-layouts  3.33 us (3%)
    pallas_call x1, Pallas kernels, body(): pl.pallas_call(functools.partial(kernel, scale), out_shape=(jax.ShapeDtyp...  111 us
    unnamed x4, local copies, waits for them, and re-layouts  3.33 us

profile of v2, /device:TPU:1, one launch (start us, length us, event | category | flops | bytes accessed | tf_op | source)
XLA Modules:
  0.0 115.1 jit_solution(8359953748390856577)
XLA Ops:
  0.6 111.1 %shard_map.77 = (bf16[16,192,256]{2,1,0:T(8,128)(2,1)}, f32[12,3,192]{2,1,0:T(4,128)}) custom-call(bf16[16,256,768]{2,1,0:T(8,128)(2,1)} %sheet_h.1, bf16[192,768]{1,0:T(8,128)(2,1)} %bitcast.9, bf16[192,768]{1,0:T(8,128)(2,1)} %bitcast.10, bf16[192,768]{1,0:T(8,128)(2,1)} %bitcast.11, bf16[16,3,64,256]{3,2,1,0:T(8,128)(2,1)} %bitcast.8, s32[16]{0:T(128)} %lens.1), custom_call_target="tpu_custom_call" | custom-call | tf_op jit(solution)/shard_map/pallas_call | solution.py:401
  111.7 0.0 copy-start
  111.8 2.7 %copy.10 = bf16[16,256,192]{1,2,0:T(8,128)(2,1)} copy(bf16[16,256,192]{1,2,0:T(8,128)(2,1)} %bitcast.7) | data formatting | bytes 3145728
  114.5 0.0 copy-done
  114.5 0.6 copy.11
Async XLA Ops:
  111.7 2.7 %copy-start = (f32[12,3,192]{2,1,0:T(4,128)S(1)}, f32[12,3,192]{2,1,0:T(4,128)}, u32[]{:S(2)}) copy-start(f32[12,3,192]{2,1,0:T(4,128)} %get-tuple-element.9) | copy-start | bytes 82948

commit v3 on v2

v3 whole, which is shorter than its diff:
```python
import functools

import jax
import jax.numpy as jnp
from jax import lax
from jax.experimental import pallas as pl
from jax.experimental.pallas import tpu as pltpu
from jax.sharding import PartitionSpec as P

HEAD_DIM = 64
MESH = pl.DeviceIdType.MESH
NX, NZ, NY = 4, 8, 4
NH = 3
F32 = jnp.float32
BF16 = jnp.bfloat16


def nt(a, b):
    return lax.dot_general(a, b, (((1,), (1,)), ((), ())), preferred_element_type=F32)


def nn(a, b):
    return lax.dot_general(a, b, (((1,), (0,)), ((), ())), preferred_element_type=F32)


def tn(a, b):
    return lax.dot_general(a, b, (((0,), (0,)), ((), ())), preferred_element_type=F32)


def kernel(
    scale,
    sheet_h, wq, wk, wv, cot_h, lens, out_h, wg_out,
    sheet, w_t, w_c, w_vc, vm, q_t, k_t, v_t, g_t,
    w_far, wv_far, w_out, q_far, k_far, g_far,
    u, a_recv, a_sum, x_recv, x_sum, z_recv, full, gat, gat_far, prob, dsc,
    acc, out_v, wg_acc, wg_n, wg_b, wa_recv, wx_recv, wx_sum, wz_recv,
    s_sheet, s_cot, s_w, s_out,
    sa, ra, sx, rx, sz, rz, sd, rd, sgz, rgz, sgx, rgx, sgc, rgc,
    swy, rwy, sww, rww, swc, rwc, sg, rg, sgr, rgr, sty, rty, soz, roz, sox, rox, soc, roc,
    swa, rwa, swx, rwx, swz, rwz,
):
    ri = lax.axis_index("rows")
    y = lax.axis_index("heads")
    core = lax.rem(ri, 2)
    x = lax.rem(ri // 2, NX)
    z = ri // (2 * NX)
    other = 1 - core
    block = x * NZ + z
    partner = {"rows": (z * NX + x) * 2 + other}
    xs = [lax.rem(x + k, NX) for k in range(1, NX)]
    zs = [lax.rem(z + k, NZ) for k in range(1, NZ)]
    ys = [lax.rem(y + k, NY) for k in range(1, NY)]
    xpeer = [{"rows": (z * NX + xk) * 2 + core} for xk in xs]
    zpeer = [{"rows": (zk * NX + x) * 2 + core} for zk in zs]
    ypeer = [{"heads": yk} for yk in ys]
    d_up, d_dn = ypeer[0], ypeer[2]

    def remote(src, dst, ss, rs, dev):
        return pltpu.make_async_remote_copy(
            src_ref=src, dst_ref=dst, send_sem=ss, recv_sem=rs, device_id=dev, device_id_type=MESH
        )

    sends = []

    def send(copies):
        for c in copies:
            c.start()
        sends.extend(copies)

    def receive(copies):
        for c in copies:
            c.wait_recv()

    def w_copy(t):
        return pltpu.make_async_copy((wq, wk, wv)[t], w_t.at[192 * t:192 * t + 192], s_w.at[t])

    def sheet_copy(r):
        return pltpu.make_async_copy(sheet_h.at[r], sheet.at[r], s_sheet.at[r])

    def cot_copy(r):
        at = pl.multiple_of(r * 64, 64)
        return pltpu.make_async_copy(cot_h.at[r], g_t.at[:, pl.ds(at, 64), :], s_cot.at[r])

    w_copy(2).start()
    for r in range(16):
        sheet_copy(r).start()
    w_copy(0).start()
    w_copy(1).start()
    for r in range(16):
        cot_copy(r).start()

    barrier = pltpu.get_barrier_semaphore()
    peers = [partner] + ypeer + xpeer + zpeer
    for dev in peers:
        pl.semaphore_signal(barrier, inc=1, device_id=dev, device_id_type=MESH)

    for r in range(16):
        vm[r:r + 1, :] = (lax.broadcasted_iota(jnp.int32, (1, 256), 1) < lens[r]).astype(F32)

    def split_rows(ref, r, mat):
        at = pl.multiple_of(r * 64, 64)
        for h in range(NH):
            ref[h, pl.ds(at, 64), :] = mat[h * 64:(h + 1) * 64].astype(BF16)

    def value_rows(i, _):
        for n in range(4):
            sheet_copy(4 * i + n).wait()
        mat = nt(w_t[384:576], sheet[pl.ds(4 * i, 4)].reshape(1024, 768))
        for n in range(4):
            split_rows(v_t, 4 * i + n, mat[:, 256 * n:256 * n + 256] * vm[pl.ds(4 * i + n, 1), :])
        return 0

    w_copy(2).wait()
    w_vc[...] = w_t[384:576].T
    lax.fori_loop(0, 4, value_rows, 0)
    for r in range(16):
        cot_copy(r).wait()
    w_copy(0).wait()
    w_copy(1).wait()

    def wy_copies():
        got = []
        for k in range(NY - 1):
            src = w_t.at[pl.ds(pl.multiple_of(core * 192 + x * 48, 16), 48), :]
            got.append(remote(src, w_far.at[k, core, x], swy.at[0, k], rwy.at[0, k], ypeer[k]))
            src = w_vc.at[pl.ds(pl.multiple_of(ys[k] * 192 + x * 48, 16), 48), :]
            got.append(remote(src, wv_far.at[k, x], swy.at[1, k], rwy.at[1, k], ypeer[k]))
        return got

    def wx_copies():
        got = []
        for k in range(NX - 1):
            ref = w_far.at[:, core, x]
            got.append(remote(ref, ref, sww.at[0, k], rww.at[0, k], xpeer[k]))
            ref = wv_far.at[:, x]
            got.append(remote(ref, ref, sww.at[1, k], rww.at[1, k], xpeer[k]))
        return got

    def near_copies(c):
        src = g_t.at[:, 128 * c:128 * c + 128, :]
        return [
            remote(src, g_far.at[0, :, 128 * c:128 * c + 128, :], sg.at[0, c], rg.at[0, c], d_up),
            remote(src, g_far.at[2, :, 128 * c:128 * c + 128, :], sg.at[1, c], rg.at[1, c], d_dn),
        ]

    def relay_copies(c):
        lo, hi = 128 * c, 128 * c + 64
        return [
            remote(
                g_far.at[0, :, lo:lo + 64, :], g_far.at[1, :, lo:lo + 64, :], sgr.at[0, c], rgr.at[0, c], d_up
            ),
            remote(
                g_far.at[2, :, hi:hi + 64, :], g_far.at[1, :, hi:hi + 64, :], sgr.at[1, c], rgr.at[1, c], d_dn
            ),
        ]

    def near(chunks):
        for c in chunks:
            for cp in near_copies(c):
                cp.start()

    def relay(chunks):
        for c in chunks:
            for got, cp in zip(near_copies(c), relay_copies(c)):
                got.wait_recv()
                cp.start()

    def core_copy(t, h):
        return remote(
            u.at[t, other, h], a_recv.at[t, h], sa.at[t, h], ra.at[t, h], partner
        )

    def x_copy(t, k):
        at = pl.multiple_of(xs[k] * 64, 64)
        return remote(
            a_sum.at[t, :, pl.ds(at, 64), :], x_recv.at[t, k], sx.at[t, k], rx.at[t, k], xpeer[k]
        )

    def z_copy(t, k):
        at = pl.multiple_of(zs[k] * 8, 8)
        return remote(
            x_sum.at[t, :, pl.ds(at, 8), :], z_recv.at[t, k], sz.at[t, k], rz.at[t, k], zpeer[k]
        )

    def outer(t, left, right):
        def one(h, _):
            mat = tn(left[h], right[h])
            u[t, 0, h] = mat[:, :128]
            u[t, 1, h] = mat[:, 128:]
            core_copy(t, h).start()
            return 0

        lax.fori_loop(0, NH, one, 0)
        sends.extend(core_copy(t, h) for h in range(NH))

    def add_core(t):
        for h in range(NH):
            core_copy(t, h).wait_recv()
            a_sum[t, h] = u[t, core, h] + a_recv[t, h]
        send([x_copy(t, k) for k in range(NX - 1)])

    def add_x(t):
        receive([x_copy(t, k) for k in range(NX - 1)])
        mine = pl.multiple_of(x * 64, 64)
        x_sum[t] = a_sum[t, :, pl.ds(mine, 64), :] + x_recv[t, 0] + x_recv[t, 1] + x_recv[t, 2]
        send([z_copy(t, k) for k in range(NZ - 1)])

    def add_z(t):
        receive([z_copy(t, k) for k in range(NZ - 1)])
        mine = pl.multiple_of(z * 8, 8)
        total = x_sum[t, :, pl.ds(mine, 8), :]
        for k in range(NZ - 1):
            total = total + z_recv[t, k]
        full[core, t] = total

    def query_rows(qr, kr, weights, lo, hi):
        def one(i, _):
            mat = nt(weights(), sheet[pl.ds(4 * i, 4)].reshape(1024, 768))
            for n in range(4):
                sub = mat[:, 256 * n:256 * n + 256] * vm[pl.ds(4 * i + n, 1), :]
                split_rows(qr, 4 * i + n, sub[:192])
                split_rows(kr, 4 * i + n, sub[192:])
            return 0

        lax.fori_loop(lo, hi, one, 0)

    def own_weights():
        return w_t[0:384]

    pl.semaphore_wait(barrier, len(peers))
    send(wy_copies())
    near([0, 1, 2])
    outer(0, g_t, v_t)
    query_rows(q_t, k_t, own_weights, 0, 1)
    add_core(0)
    query_rows(q_t, k_t, own_weights, 1, 4)
    outer(1, q_t, k_t)
    near([3, 4])
    add_core(1)
    receive(wy_copies())
    send(wx_copies())
    add_x(0)
    rows_y = pl.ds(pl.multiple_of(y * 192, 16), 192)
    w_c[...] = w_t[0:384].T
    w_out[0, :, 0:384] = w_c[rows_y, :]
    w_out[0, :, 384:576] = w_vc[rows_y, :]
    relay([0])
    add_x(1)
    add_z(0)
    add_z(1)

    half_copy = remote(full.at[core], full.at[core], sd.at[0], rd.at[0], partner)
    send([half_copy])
    half_copy.wait_recv()

    dprob = jnp.concatenate([full[0, 0], full[1, 0]], axis=-1)
    logits = jnp.concatenate([full[0, 1], full[1, 1]], axis=-1) * scale
    top = jnp.max(logits, axis=-1, keepdims=True)
    ex = jnp.exp(logits - top)
    probs = ex / jnp.sum(ex, axis=-1, keepdims=True)
    inner = jnp.sum(probs * dprob, axis=-1, keepdims=True)
    dscore = scale * probs * (dprob - inner)
    tile = jnp.concatenate([probs, dscore], axis=1)
    gat[core, block] = jnp.where(core == 0, tile[:, :, :128], tile[:, :, 128:]).astype(BF16)

    own = gat.at[core, block]
    gz = [remote(own, own, sgz.at[k], rgz.at[k], zpeer[k]) for k in range(NZ - 1)]
    ty = [
        remote(own, gat_far.at[k, core, block], sty.at[k], rty.at[k], ypeer[k]) for k in range(NY - 1)
    ]
    send(gz)
    send(ty)
    near([5, 6, 7])

    xblock = pl.ds(pl.multiple_of(x * NZ, NZ), NZ)

    def gx_copy(k):
        src = gat.at[core, xblock]
        return remote(src, src, sgx.at[k], rgx.at[k], xpeer[k])

    def from_x(k):
        return pl.ds(pl.multiple_of(lax.rem(x + NX - k, NX) * NZ, NZ), NZ)

    def gc_copy(k):
        src = gat.at[core, from_x(k)]
        return remote(src, src, sgc.at[k], rgc.at[k], partner)

    def oz_copy(k):
        src = gat_far.at[:, core, block]
        return remote(src, src, soz.at[k], roz.at[k], zpeer[k])

    def ox_copy(s, k):
        src = gat_far.at[s, core, xblock]
        return remote(src, src, sox.at[s, k], rox.at[s, k], xpeer[k])

    def oc_copy(s, k):
        src = gat_far.at[s, core, from_x(k)]
        return remote(src, src, soc.at[s, k], roc.at[s, k], partner)

    receive(wx_copies())
    wc_copy = remote(w_far.at[:, core], w_far.at[:, core], swc.at[0], rwc.at[0], partner)
    send([wc_copy])
    receive(gz)
    send([gx_copy(k) for k in range(NX - 1)])
    send([gc_copy(0)])
    receive(ty)
    send([oz_copy(k) for k in range(NZ - 1)])
    wc_copy.wait_recv()

    def far_weights(s):
        w_c[...] = w_far[s].reshape(384, 768).T
        w_out[s + 1, :, 0:384] = w_c[rows_y, :]
        w_out[s + 1, :, 384:576] = wv_far[s].reshape(192, 192)

    def far_rows(s):
        query_rows(q_far.at[s], k_far.at[s], lambda: w_far[s].reshape(384, 768), 0, 4)

    far_weights(0)
    far_rows(0)
    relay([1, 2])
    for k in range(NX - 1):
        gx_copy(k).wait_recv()
        send([gc_copy(k + 1)])
    receive([oz_copy(k) for k in range(NZ - 1)])
    send([ox_copy(s, k) for s in range(NY - 1) for k in range(NX - 1)])
    send([oc_copy(s, 0) for s in range(NY - 1)])
    receive([gc_copy(k) for k in range(NX)])

    def unpack(src):
        def one(h, _):
            for ch in range(2):
                mat = src(ch, h).astype(F32)
                prob[h, :, ch * 128:(ch + 1) * 128] = mat[:, :8].reshape(256, 128).astype(BF16)
                dsc[h, :, ch * 128:(ch + 1) * 128] = mat[:, 8:].reshape(256, 128).astype(BF16)
            return 0

        lax.fori_loop(0, NH, one, 0)

    def masked(ref, h, mat):
        for r in range(16):
            ref[h, r * 64:(r + 1) * 64, :] = (mat[r * 64:(r + 1) * 64] * vm[r:r + 1, :]).astype(BF16)

    def back_qk(qr, kr):
        def one(h, _):
            dq = nt(kr[h], dsc[h])
            dk = nn(qr[h], dsc[h])
            masked(qr, h, dq)
            masked(kr, h, dk)
            return 0

        lax.fori_loop(0, NH, one, 0)

    def gathered(refs, c):
        cols = []
        for n in range(4):
            at = pl.multiple_of(c * 256 + n * 64, 64)
            cols.append(jnp.concatenate([ref[h, pl.ds(at, 64), :] for ref in refs for h in range(NH)], axis=0))
        return jnp.concatenate(cols, axis=1)

    unpack(lambda ch, h: gat[ch, :, h])
    back_qk(q_t, k_t)

    def back_v(h, _):
        masked(v_t, h, nn(g_t[h], prob[h]))
        return 0

    lax.fori_loop(0, NH, back_v, 0)
    relay([3])
    wg_acc[...] = jnp.zeros_like(wg_acc)

    def own_chunk(c, _):
        grads = gathered((q_t, k_t, v_t), c)
        acc[c] = nn(w_out[0], grads)
        wg_acc[...] += nn(grads, sheet[pl.ds(4 * c, 4)].reshape(1024, 768))
        return 0

    lax.fori_loop(0, 4, own_chunk, 0)
    wg_n[0:768] = wg_acc[...].T
    wg_n[768:784] = jnp.zeros((16, 576), F32)
    for g in range(64):
        gc, gx, gz_ = g % 2, (g // 2) % NX, g // (2 * NX)
        wg_b[gc, gx, gz_] = wg_n[12 * g:12 * g + 16, :].astype(BF16)
    wa = remote(wg_b.at[other], wa_recv, swa.at[0], rwa.at[0], partner)
    send([wa])
    relay([4, 5])

    def far_ready(s):
        for k in range(NX - 1):
            ox_copy(s, k).wait_recv()
            send([oc_copy(s, k + 1)])

    def wx_copy(k):
        return remote(wa_recv.at[xs[k]], wx_recv.at[k], swx.at[k], rwx.at[k], xpeer[k])

    def wz_copy(k):
        return remote(wx_sum.at[zs[k]], wz_recv.at[k], swz.at[k], rwz.at[k], zpeer[k])

    def far_qk(s):
        receive([oc_copy(s, k) for k in range(NX)])
        unpack(lambda ch, h: gat_far[s, ch, :, h])
        back_qk(q_far.at[s], k_far.at[s])

    def far_qk_out(s):
        def one(c, _):
            acc[c] += nn(w_out[s + 1, :, 0:384], gathered((q_far.at[s], k_far.at[s]), c))
            return 0

        lax.fori_loop(0, 4, one, 0)

    def far_v(s, h, c):
        at = pl.multiple_of(c * 256, 256)
        mat = nn(g_far[s, h, pl.ds(at, 256), :], prob[h])
        return [
            (mat[n * 64:(n + 1) * 64] * vm[pl.ds(4 * c + n, 1), :]).astype(BF16) for n in range(4)
        ]

    def far_v_mat(s, c):
        parts = [far_v(s, h, c) for h in range(NH)]
        return jnp.concatenate(
            [jnp.concatenate([parts[h][n] for h in range(NH)], axis=0) for n in range(4)], axis=1
        )

    def far_v_out(s):
        def one(c, _):
            acc[c] += nn(w_out[s + 1, :, 384:576], far_v_mat(s, c))
            return 0

        lax.fori_loop(0, 4, one, 0)

    far_weights(1)
    far_rows(1)
    far_ready(0)
    far_qk(0)
    relay([6, 7])
    far_qk_out(0)
    far_v_out(0)

    wa.wait_recv()
    wa_recv[...] = (wa_recv[...].astype(F32) + wg_b[core].astype(F32)).astype(BF16)
    send([wx_copy(k) for k in range(NX - 1)])

    far_weights(2)
    far_rows(2)
    far_ready(2)
    far_qk(2)
    far_qk_out(2)
    far_v_out(2)

    receive([wx_copy(k) for k in range(NX - 1)])
    wx_sum[...] = (
        wa_recv[x].astype(F32) + wx_recv[0].astype(F32) + wx_recv[1].astype(F32) + wx_recv[2].astype(F32)
    ).astype(BF16)
    send([wz_copy(k) for k in range(NZ - 1)])

    far_ready(1)
    far_qk(1)
    far_qk_out(1)

    def out_copy(c):
        rows = pl.ds(4 * c, 4)
        return pltpu.make_async_copy(out_v.at[rows], out_h.at[rows], s_out.at[c])

    for c in range(4):
        for cc in (2 * c, 2 * c + 1):
            receive(relay_copies(cc))
        tot = acc[c] + nn(w_out[2, :, 384:576], far_v_mat(1, c))
        for n in range(4):
            out_v[4 * c + n] = tot[:, 256 * n:256 * n + 256].astype(BF16)
        out_copy(c).start()

    receive([wz_copy(k) for k in range(NZ - 1)])
    total = wx_sum[z].astype(F32)
    for k in range(NZ - 1):
        total = total + wz_recv[k].astype(F32)
    for t in range(3):
        wg_out[:, t, :] = total[:12, 192 * t:192 * t + 192]

    for c in range(8):
        for cp in near_copies(c) + relay_copies(c):
            cp.wait_send()
    for cp in sends:
        cp.wait_send()
    for c in range(4):
        out_copy(c).wait()


def body(sheet, w_query, w_key, w_value, cotangent, lengths):
    scale = float((HEAD_DIM * sheet.shape[0] * lax.axis_size("rows")) ** -0.5)
    vmem = pl.BlockSpec(memory_space=pltpu.VMEM)
    anyw = pl.BlockSpec(memory_space=pl.ANY)
    dma = pltpu.SemaphoreType.DMA
    V = pltpu.VMEM
    rows = (3, 1024, 256)
    scratch = [
        V((16, 256, 768), BF16), V((576, 768), BF16), V((768, 384), BF16), V((768, 192), BF16), V((16, 256), F32),
        V(rows, BF16), V(rows, BF16), V(rows, BF16), V(rows, BF16),
        V((3, 2, 4, 48, 768), BF16), V((3, 4, 48, 192), BF16), V((4, 192, 576), BF16),
        V((3,) + rows, BF16), V((3,) + rows, BF16), V((3,) + rows, BF16),
        V((2, 2, 3, 256, 128), F32), V((2, 3, 256, 128), F32), V((2, 3, 256, 128), F32),
        V((2, 3, 3, 64, 128), F32), V((2, 3, 64, 128), F32),
        V((2, 7, 3, 8, 128), F32), V((2, 2, 3, 8, 128), F32),
        V((2, 32, 3, 16, 128), BF16), V((3, 2, 32, 3, 16, 128), BF16),
        V((3, 256, 256), BF16), V((3, 256, 256), BF16),
        V((4, 192, 1024), F32), V((16, 192, 256), BF16),
        V((576, 768), F32), V((784, 576), F32), V((2, 4, 8, 16, 576), BF16), V((4, 8, 16, 576), BF16),
        V((3, 8, 16, 576), BF16), V((8, 16, 576), BF16), V((7, 16, 576), BF16),
        dma((16,)), dma((16,)), dma((3,)), dma((4,)),
    ]
    shapes = [
        (2, 3), (2, 3), (2, 7), (1,), (7,), (3,), (4,),
        (2, 3), (2, 3), (1,), (2, 8), (2, 8), (3,), (7,), (3, 3), (3, 4),
        (1,), (3,), (7,),
    ]
    for shape in shapes:
        scratch += [dma(shape), dma(shape)]
    out, wg = pl.pallas_call(
        functools.partial(kernel, scale),
        out_shape=(jax.ShapeDtypeStruct((16, 192, 256), BF16), jax.ShapeDtypeStruct((12, 3, 192), F32)),
        in_specs=[anyw] * 5 + [pl.BlockSpec(memory_space=pltpu.SMEM)],
        out_specs=(anyw, vmem),
        scratch_shapes=scratch,
        compiler_params=pltpu.CompilerParams(
            collective_id=0, has_side_effects=True, vmem_limit_bytes=62 * 1024 * 1024
        ),
    )(
        sheet, w_query.T, w_key.T, w_value.T,
        cotangent.transpose(0, 2, 1).reshape(16, NH, HEAD_DIM, 256), lengths,
    )
    return out.transpose(0, 2, 1), wg


def solution(mesh):
    in_specs = (
        P("rows", None, None),
        P(None, "heads"),
        P(None, "heads"),
        P(None, "heads"),
        P("rows", None, "heads"),
        P("rows"),
    )
    out_specs = (P("rows", None, "heads"), P("rows", None, "heads"))
    return jax.shard_map(body, mesh=mesh, in_specs=in_specs, out_specs=out_specs, check_vma=False)
```

time: 115 us -> 96.8 us (0.84)
  Pallas kernels: 111 us -> 92.8 us
    pallas_call x1, Pallas kernels: 111 us -> 92.8 us  [body(): pl.pallas_call(functools.partial(kernel, scale), out_shape=(jax.ShapeDtyp...]
where the time goes in v3:
time: 96.8 us; the launch traced here: 96.7 us
  Pallas kernels  92.8 us (96%)
  local copies, waits for them, and re-layouts  3.33 us (3%)
    pallas_call x1, Pallas kernels, body(): pl.pallas_call(functools.partial(kernel, scale), out_shape=(jax.ShapeDtyp...  92.8 us
    unnamed x4, local copies, waits for them, and re-layouts  3.33 us

profile of v3, /device:TPU:1, one launch (start us, length us, event | category | flops | bytes accessed | tf_op | source)
XLA Modules:
  0.0 96.7 jit_solution(16113485778344709133)
XLA Ops:
  0.6 92.8 %shard_map.77 = (bf16[16,192,256]{2,1,0:T(8,128)(2,1)}, f32[12,3,192]{2,1,0:T(4,128)}) custom-call(bf16[16,256,768]{2,1,0:T(8,128)(2,1)} %sheet_h.1, bf16[192,768]{1,0:T(8,128)(2,1)} %bitcast.9, bf16[192,768]{1,0:T(8,128)(2,1)} %bitcast.10, bf16[192,768]{1,0:T(8,128)(2,1)} %bitcast.11, bf16[16,3,64,256]{3,2,1,0:T(8,128)(2,1)} %bitcast.8, s32[16]{0:T(128)} %lens.1), custom_call_target="tpu_custom_call" | custom-call | tf_op jit(solution)/shard_map/pallas_call | solution.py:516
  93.4 0.0 copy-start
  93.4 2.7 %copy.10 = bf16[16,256,192]{1,2,0:T(8,128)(2,1)} copy(bf16[16,256,192]{1,2,0:T(8,128)(2,1)} %bitcast.7) | data formatting | bytes 3145728
  96.1 0.0 copy-done
  96.1 0.6 copy.11
Async XLA Ops:
  93.4 2.7 %copy-start = (f32[12,3,192]{2,1,0:T(4,128)S(1)}, f32[12,3,192]{2,1,0:T(4,128)}, u32[]{:S(2)}) copy-start(f32[12,3,192]{2,1,0:T(4,128)} %get-tuple-element.9) | copy-start | bytes 82948

commit v4 on v3

v4 whole, which is shorter than its diff:
```python
import functools

import jax
import jax.numpy as jnp
from jax import lax
from jax.experimental import pallas as pl
from jax.experimental.pallas import tpu as pltpu
from jax.sharding import PartitionSpec as P

HEAD_DIM = 64
MESH = pl.DeviceIdType.MESH
NX, NZ, NY = 4, 8, 4
NH = 3
F32 = jnp.float32
BF16 = jnp.bfloat16


def nt(a, b):
    return lax.dot_general(a, b, (((1,), (1,)), ((), ())), preferred_element_type=F32)


def nn(a, b):
    return lax.dot_general(a, b, (((1,), (0,)), ((), ())), preferred_element_type=F32)


def tn(a, b):
    return lax.dot_general(a, b, (((0,), (0,)), ((), ())), preferred_element_type=F32)


def kernel(
    scale,
    sheet_h, wq, wk, wv, cot_h, lens, out_h, wg_out,
    sheet, w_t, w_c, w_vc, vm, q_t, k_t, v_t, g_t,
    w_far, wv_far, w_out, q_far, k_far, g_far,
    u, a_recv, a_sum, x_recv, x_sum, z_recv, full, gat, gat_far, prob, dsc,
    acc, out_v, wg_acc, wg_n, wg_b, wa_recv, wz_recv, wx_f, wx_sum, wx_recv,
    s_sheet, s_cot, s_w, s_out,
    sa, ra, sx, rx, sz, rz, sd, rd, sgz, rgz, sgx, rgx, sgc, rgc,
    swy, rwy, sww, rww, swc, rwc, sg, rg, sgr, rgr, sty, rty, soz, roz, sox, rox, soc, roc,
    swa, rwa, swx, rwx, swz, rwz,
):
    ri = lax.axis_index("rows")
    y = lax.axis_index("heads")
    core = lax.rem(ri, 2)
    x = lax.rem(ri // 2, NX)
    z = ri // (2 * NX)
    other = 1 - core
    block = x * NZ + z
    partner = {"rows": (z * NX + x) * 2 + other}
    xs = [lax.rem(x + k, NX) for k in range(1, NX)]
    zs = [lax.rem(z + k, NZ) for k in range(1, NZ)]
    ys = [lax.rem(y + k, NY) for k in range(1, NY)]
    xpeer = [{"rows": (z * NX + xk) * 2 + core} for xk in xs]
    zpeer = [{"rows": (zk * NX + x) * 2 + core} for zk in zs]
    ypeer = [{"heads": yk} for yk in ys]
    d_up, d_dn = ypeer[0], ypeer[2]

    def remote(src, dst, ss, rs, dev):
        return pltpu.make_async_remote_copy(
            src_ref=src, dst_ref=dst, send_sem=ss, recv_sem=rs, device_id=dev, device_id_type=MESH
        )

    sends = []

    def send(copies):
        for c in copies:
            c.start()

    def sent(ref, sem):
        sends.append((ref, sem))

    def flush():
        for ref, sem in sends:
            remote(ref, ref, sem, sem, partner).wait_send()

    def arrived(ref, sem):
        remote(ref, ref, sem, sem, partner).wait_recv()

    def w_copy(t):
        return pltpu.make_async_copy((wq, wk, wv)[t], w_t.at[192 * t:192 * t + 192], s_w.at[0])

    def sheet_copy(i):
        rows = pl.ds(4 * i, 4)
        return pltpu.make_async_copy(sheet_h.at[rows], sheet.at[rows], s_sheet.at[i])

    def cot_copy(r):
        return pltpu.make_async_copy(cot_h.at[r], g_t.at[:, 64 * r:64 * r + 64, :], s_cot.at[0])

    for t in range(3):
        w_copy(t).start()
    for i in range(4):
        sheet_copy(i).start()

    barrier = pltpu.get_barrier_semaphore()
    peers = [partner] + ypeer + xpeer + zpeer
    for dev in peers:
        pl.semaphore_signal(barrier, inc=1, device_id=dev, device_id_type=MESH)

    for r in range(16):
        vm[r:r + 1, :] = (lax.broadcasted_iota(jnp.int32, (1, 256), 1) < lens[r]).astype(F32)

    def split_rows(ref, r, mat):
        at = pl.multiple_of(r * 64, 64)
        for h in range(NH):
            ref[h, pl.ds(at, 64), :] = mat[h * 64:(h + 1) * 64].astype(BF16)

    def value_rows(i, _):
        sheet_copy(i).wait()
        mat = nt(w_t[384:576], sheet[pl.ds(4 * i, 4)].reshape(1024, 768))
        for n in range(4):
            split_rows(v_t, 4 * i + n, mat[:, 256 * n:256 * n + 256] * vm[pl.ds(4 * i + n, 1), :])
        return 0

    pltpu.make_async_copy(w_t, w_t, s_w.at[0]).wait()
    for r in range(16):
        cot_copy(r).start()
    w_vc[...] = w_t[384:576].T
    lax.fori_loop(0, 2, value_rows, 0)
    pl.semaphore_wait(barrier, len(peers))

    quarter = lax.rem(z, 4)
    piece = [quarter, x, x]

    def wy_copies():
        got = []
        for k in range(NY - 1):
            p = piece[k]
            src = w_t.at[pl.ds(pl.multiple_of(core * 192 + p * 48, 16), 48), :]
            got.append(remote(src, w_far.at[k, core, p], swy.at[0], rwy.at[0], ypeer[k]))
            src = w_vc.at[pl.ds(pl.multiple_of(ys[k] * 192 + p * 48, 16), 48), :]
            got.append(remote(src, wv_far.at[k, p], swy.at[1], rwy.at[1], ypeer[k]))
        return got

    hop2 = lax.rem(z + 2 + 4 * lax.rem(z, 2), NZ)
    wpeer = [zpeer[0], zpeer[NZ - 2], {"rows": (hop2 * NX + x) * 2 + core}]

    def wz_copies():
        got = []
        for k in range(3):
            ref = w_far.at[0, core, quarter]
            got.append(remote(ref, ref, sww.at[0], rww.at[0], wpeer[k]))
            ref = wv_far.at[0, quarter]
            got.append(remote(ref, ref, sww.at[1], rww.at[1], wpeer[k]))
        return got

    def wx_copies():
        got = []
        for k in range(3):
            ref = w_far.at[1:3, core, x]
            got.append(remote(ref, ref, sww.at[2], rww.at[2], xpeer[k]))
            ref = wv_far.at[1:3, x]
            got.append(remote(ref, ref, sww.at[3], rww.at[3], xpeer[k]))
        return got

    def near_copies(c):
        src = g_t.at[:, 128 * c:128 * c + 128, :]
        return [
            remote(src, g_far.at[0, :, 128 * c:128 * c + 128, :], sg.at[0], rg.at[0, c], d_up),
            remote(src, g_far.at[2, :, 128 * c:128 * c + 128, :], sg.at[1], rg.at[1, c], d_dn),
        ]

    def relay_copies(c):
        lo, hi = 128 * c, 128 * c + 64
        return [
            remote(
                g_far.at[0, :, lo:lo + 64, :], g_far.at[1, :, lo:lo + 64, :], sgr.at[0], rgr.at[c // 2], d_up
            ),
            remote(
                g_far.at[2, :, hi:hi + 64, :], g_far.at[1, :, hi:hi + 64, :], sgr.at[1], rgr.at[c // 2], d_dn
            ),
        ]

    def near(chunks):
        for c in chunks:
            for cp in near_copies(c):
                cp.start()

    def relay(chunks):
        for c in chunks:
            for got, cp in zip(near_copies(c), relay_copies(c)):
                got.wait_recv()
                cp.start()

    def core_copy(t, h):
        return remote(
            u.at[t, other, h], a_recv.at[t, h], sa.at[t], ra.at[t], partner
        )

    def x_copy(t, k):
        at = pl.multiple_of(xs[k] * 64, 64)
        return remote(
            a_sum.at[t, :, pl.ds(at, 64), :], x_recv.at[t, k], sx.at[t], rx.at[t], xpeer[k]
        )

    def z_copy(t, k):
        at = pl.multiple_of(zs[k] * 8, 8)
        return remote(
            x_sum.at[t, :, pl.ds(at, 8), :], z_recv.at[t, k], sz.at[t], rz.at[t], zpeer[k]
        )

    def outer(t, left, right):
        def one(h, _):
            mat = tn(left[h], right[h])
            u[t, 0, h] = mat[:, :128]
            u[t, 1, h] = mat[:, 128:]
            core_copy(t, h).start()
            return 0

        lax.fori_loop(0, NH, one, 0)
        sent(a_recv.at[t], sa.at[t])

    def add_core(t):
        arrived(a_recv.at[t], ra.at[t])
        a_sum[t] = u[t, core] + a_recv[t]
        send([x_copy(t, k) for k in range(NX - 1)])
        sent(x_recv.at[t], sx.at[t])

    def add_x(t):
        arrived(x_recv.at[t], rx.at[t])
        mine = pl.multiple_of(x * 64, 64)
        x_sum[t] = a_sum[t, :, pl.ds(mine, 64), :] + x_recv[t, 0] + x_recv[t, 1] + x_recv[t, 2]
        send([z_copy(t, k) for k in range(NZ - 1)])
        sent(z_recv.at[t], sz.at[t])

    def add_z(t):
        arrived(z_recv.at[t], rz.at[t])
        mine = pl.multiple_of(z * 8, 8)
        total = x_sum[t, :, pl.ds(mine, 8), :]
        for k in range(NZ - 1):
            total = total + z_recv[t, k]
        full[core, t] = total

    def query_rows(qr, kr, weights, lo, hi):
        def one(i, _):
            mat = nt(weights(), sheet[pl.ds(4 * i, 4)].reshape(1024, 768))
            for n in range(4):
                sub = mat[:, 256 * n:256 * n + 256] * vm[pl.ds(4 * i + n, 1), :]
                split_rows(qr, 4 * i + n, sub[:192])
                split_rows(kr, 4 * i + n, sub[192:])
            return 0

        lax.fori_loop(lo, hi, one, 0)

    def own_weights():
        return w_t[0:384]

    def far_weights(s):
        w_c[...] = w_far[s].reshape(384, 768).T
        w_out[s + 1, :, 0:384] = w_c[rows_y, :]
        w_out[s + 1, :, 384:576] = wv_far[s].reshape(192, 192)

    def far_rows(s):
        far_weights(s)
        query_rows(q_far.at[s], k_far.at[s], lambda: w_far[s].reshape(384, 768), 0, 4)

    send(wy_copies())
    sent(w_far.at[:, 0, 0], swy.at[0])
    sent(wv_far.at[:, 0], swy.at[1])
    lax.fori_loop(2, 4, value_rows, 0)
    pltpu.make_async_copy(g_t, g_t, s_cot.at[0]).wait()
    near([0, 1, 2])
    outer(0, g_t, v_t)
    query_rows(q_t, k_t, own_weights, 0, 1)
    add_core(0)
    query_rows(q_t, k_t, own_weights, 1, 4)
    outer(1, q_t, k_t)
    near([3])
    add_core(1)
    arrived(w_far.at[:, 0, 0], rwy.at[0])
    arrived(wv_far.at[:, 0], rwy.at[1])
    send(wz_copies())
    send(wx_copies())
    sent(w_far.at[:, 0, 0], sww.at[0])
    sent(wv_far.at[:, 0], sww.at[1])
    sent(w_far.at[:, :, 0], sww.at[2])
    sent(wv_far.at[:, 0:2], sww.at[3])
    add_x(0)
    rows_y = pl.ds(pl.multiple_of(y * 192, 16), 192)
    w_c[...] = w_t[0:384].T
    w_out[0, :, 0:384] = w_c[rows_y, :]
    w_out[0, :, 384:576] = w_vc[rows_y, :]
    relay([0])
    add_x(1)
    arrived(w_far.at[:, 0, 0], rww.at[0])
    arrived(wv_far.at[:, 0], rww.at[1])
    wc_copy = remote(w_far.at[0, core], w_far.at[0, core], swc.at[0], rwc.at[0], partner)
    wd_copy = remote(w_far.at[1:3, core], w_far.at[1:3, core], swc.at[1], rwc.at[1], partner)
    send([wc_copy])
    sent(w_far.at[0, 0], swc.at[0])
    wc_copy.wait_recv()
    far_rows(0)
    add_z(0)
    add_z(1)

    half_copy = remote(full.at[core], full.at[core], sd.at[0], rd.at[0], partner)
    send([half_copy])
    sent(full.at[0], sd.at[0])
    half_copy.wait_recv()

    dprob = jnp.concatenate([full[0, 0], full[1, 0]], axis=-1)
    logits = jnp.concatenate([full[0, 1], full[1, 1]], axis=-1) * scale
    top = jnp.max(logits, axis=-1, keepdims=True)
    ex = jnp.exp(logits - top)
    probs = ex / jnp.sum(ex, axis=-1, keepdims=True)
    inner = jnp.sum(probs * dprob, axis=-1, keepdims=True)
    dscore = scale * probs * (dprob - inner)
    tile = jnp.concatenate([probs, dscore], axis=1)
    gat[core, block] = jnp.where(core == 0, tile[:, :, :128], tile[:, :, 128:]).astype(BF16)

    own = gat.at[core, block]
    gz = [remote(own, own, sgz.at[0], rgz.at[0], zpeer[k]) for k in range(NZ - 1)]
    ty = [
        remote(own, gat_far.at[k, core, block], sty.at[0], rty.at[0], ypeer[k]) for k in range(NY - 1)
    ]
    send(gz)
    send(ty)
    sent(gat.at[0, 0:7], sgz.at[0])
    sent(gat_far.at[:, 0, 0], sty.at[0])
    near([4, 5, 6, 7])

    xblock = pl.ds(pl.multiple_of(x * NZ, NZ), NZ)

    def gx_copy(k):
        src = gat.at[core, xblock]
        return remote(src, src, sgx.at[0], rgx.at[k], xpeer[k])

    def from_x(k):
        return pl.ds(pl.multiple_of(lax.rem(x + NX - k, NX) * NZ, NZ), NZ)

    def gc_copy(k):
        src = gat.at[core, from_x(k)]
        return remote(src, src, sgc.at[0], rgc.at[0], partner)

    def oz_copy(k):
        src = gat_far.at[:, core, block]
        return remote(src, src, soz.at[0], roz.at[0], zpeer[k])

    def ox_copy(s, k):
        src = gat_far.at[s, core, xblock]
        return remote(src, src, sox.at[0], rox.at[s], xpeer[k])

    def oc_copy(s, k):
        src = gat_far.at[s, core, from_x(k)]
        return remote(src, src, soc.at[0], roc.at[s], partner)

    arrived(w_far.at[:, :, 0], rww.at[2])
    arrived(wv_far.at[:, 0:2], rww.at[3])
    send([wd_copy])
    sent(w_far.at[1:3, 0], swc.at[1])
    arrived(gat.at[0, 0:7], rgz.at[0])
    send([gx_copy(k) for k in range(NX - 1)])
    send([gc_copy(0)])
    arrived(gat_far.at[:, 0, 0], rty.at[0])
    send([oz_copy(k) for k in range(NZ - 1)])
    wd_copy.wait_recv()
    far_rows(1)
    far_rows(2)
    relay([1, 2])
    for k in range(NX - 1):
        gx_copy(k).wait_recv()
        send([gc_copy(k + 1)])
    sent(gat.at[0, 0:24], sgx.at[0])
    sent(gat.at[0], sgc.at[0])
    arrived(gat.at[0], rgc.at[0])

    def unpack(src):
        def one(h, _):
            for ch in range(2):
                mat = src(ch, h).astype(F32)
                prob[h, :, ch * 128:(ch + 1) * 128] = mat[:, :8].reshape(256, 128).astype(BF16)
                dsc[h, :, ch * 128:(ch + 1) * 128] = mat[:, 8:].reshape(256, 128).astype(BF16)
            return 0

        lax.fori_loop(0, NH, one, 0)

    def masked(ref, h, mat):
        for r in range(16):
            ref[h, r * 64:(r + 1) * 64, :] = (mat[r * 64:(r + 1) * 64] * vm[r:r + 1, :]).astype(BF16)

    def back_qk(qr, kr):
        def one(h, _):
            dq = nt(kr[h], dsc[h])
            dk = nn(qr[h], dsc[h])
            masked(qr, h, dq)
            masked(kr, h, dk)
            return 0

        lax.fori_loop(0, NH, one, 0)

    def gathered(refs, c):
        cols = []
        for n in range(4):
            at = pl.multiple_of(c * 256 + n * 64, 64)
            cols.append(jnp.concatenate([ref[h, pl.ds(at, 64), :] for ref in refs for h in range(NH)], axis=0))
        return jnp.concatenate(cols, axis=1)

    unpack(lambda ch, h: gat[ch, :, h])
    back_qk(q_t, k_t)

    def back_v(h, _):
        masked(v_t, h, nn(g_t[h], prob[h]))
        return 0

    lax.fori_loop(0, NH, back_v, 0)
    arrived(gat_far.at[:, 0, 0:7], roz.at[0])
    sent(gat_far.at[:, 0, 0:7], soz.at[0])
    send([ox_copy(s, k) for s in (0, 2, 1) for k in range(NX - 1)])
    send([oc_copy(s, 0) for s in range(NY - 1)])
    sent(gat_far.at[:, 0, 0:24], sox.at[0])
    sent(gat_far.at[:, 0], soc.at[0])
    relay([3])
    wg_acc[...] = jnp.zeros_like(wg_acc)

    def own_wg(c, _):
        wg_acc[...] += nn(gathered((q_t, k_t, v_t), c), sheet[pl.ds(4 * c, 4)].reshape(1024, 768))
        return 0

    def own_out(c, _):
        acc[c] = nn(w_out[0], gathered((q_t, k_t, v_t), c))
        return 0

    lax.fori_loop(0, 4, own_wg, 0)
    wg_n[...] = wg_acc[...].T
    for gc in range(2):
        for gz_ in range(NZ):
            rows = [wg_n[12 * g:12 * g + 12, :] for g in range(8 * gz_ + gc, 8 * gz_ + 8, 2)]
            wg_b[gc, gz_] = jnp.concatenate(rows, axis=0).astype(BF16)
    wa = remote(wg_b.at[other], wa_recv, swa.at[0], rwa.at[0], partner)
    send([wa])
    sent(wa_recv, swa.at[0])
    relay([4, 5])
    lax.fori_loop(0, 4, own_out, 0)

    def far_ready(s):
        arrived(gat_far.at[s, 0, 0:24], rox.at[s])
        send([oc_copy(s, k + 1) for k in range(NX - 1)])

    def wz_copy(k):
        return remote(wa_recv.at[zs[k]], wz_recv.at[k], swz.at[0], rwz.at[0], zpeer[k])

    def wx_copy(k):
        return remote(wx_sum.at[xs[k]], wx_recv.at[k], swx.at[0], rwx.at[0], xpeer[k])

    def far_qk(s):
        arrived(gat_far.at[s, 0], roc.at[s])
        unpack(lambda ch, h: gat_far[s, ch, :, h])
        back_qk(q_far.at[s], k_far.at[s])

    def far_qk_out(s):
        def one(c, _):
            acc[c] += nn(w_out[s + 1, :, 0:384], gathered((q_far.at[s], k_far.at[s]), c))
            return 0

        lax.fori_loop(0, 4, one, 0)

    def far_v(s, h, c):
        at = pl.multiple_of(c * 256, 256)
        mat = nn(g_far[s, h, pl.ds(at, 256), :], prob[h])
        return [
            (mat[n * 64:(n + 1) * 64] * vm[pl.ds(4 * c + n, 1), :]).astype(BF16) for n in range(4)
        ]

    def far_v_mat(s, c):
        parts = [far_v(s, h, c) for h in range(NH)]
        return jnp.concatenate(
            [jnp.concatenate([parts[h][n] for h in range(NH)], axis=0) for n in range(4)], axis=1
        )

    def far_out(s, lo, hi):
        def one(c, _):
            grads = jnp.concatenate([gathered((q_far.at[s], k_far.at[s]), c), far_v_mat(s, c)], axis=0)
            acc[c] += nn(w_out[s + 1], grads)
            return 0

        lax.fori_loop(lo, hi, one, 0)

    wa.wait_recv()
    wa_recv[...] = (wa_recv[...].astype(F32) + wg_b[core].astype(F32)).astype(BF16)
    send([wz_copy(k) for k in range(NZ - 1)])
    sent(wz_recv, swz.at[0])
    far_ready(0)
    far_qk(0)
    relay([6, 7])
    far_out(0, 0, 2)
    far_ready(2)
    far_out(0, 2, 4)
    far_qk(2)
    far_out(2, 0, 3)
    far_ready(1)
    far_out(2, 3, 4)
    far_qk(1)
    arrived(wz_recv, rwz.at[0])
    wsum = wa_recv[z].astype(F32)
    for k in range(NZ - 1):
        wsum = wsum + wz_recv[k].astype(F32)
    wx_f[0:48] = wsum
    wx_f[48:56] = jnp.zeros((8, 576), F32)
    for n in range(NX):
        wx_sum[n] = wx_f[12 * n:12 * n + 16, :].astype(BF16)
    send([wx_copy(k) for k in range(NX - 1)])
    sent(wx_recv, swx.at[0])

    far_qk_out(1)

    def out_copy(c):
        rows = pl.ds(4 * c, 4)
        return pltpu.make_async_copy(out_v.at[rows], out_h.at[rows], s_out.at[0])

    for c in range(4):
        arrived(g_far.at[1, :, 256 * c:256 * c + 256, :], rgr.at[c])
        tot = acc[c] + nn(w_out[2, :, 384:576], far_v_mat(1, c))
        for n in range(4):
            out_v[4 * c + n] = tot[:, 256 * n:256 * n + 256].astype(BF16)
        out_copy(c).start()

    arrived(wx_recv, rwx.at[0])
    total = wx_sum[x].astype(F32)
    for k in range(NX - 1):
        total = total + wx_recv[k].astype(F32)
    for t in range(3):
        wg_out[:, t, :] = total[:12, 192 * t:192 * t + 192]

    for n in range(2):
        sent(g_t, sg.at[n])
        sent(g_far.at[1, :, 0:512, :], sgr.at[n])
    flush()
    pltpu.make_async_copy(out_v, out_v, s_out.at[0]).wait()


def place(out_h, wg_h, out_f, wg_f, out_v, wg_v, s_in, s_out):
    def pieces(src, dst, sem):
        got = [pltpu.make_async_copy(src[1], dst[1], sem.at[4])]
        for c in range(4):
            rows = pl.ds(4 * c, 4)
            got.append(pltpu.make_async_copy(src[0].at[rows], dst[0].at[rows], sem.at[c]))
        return got

    first = pieces((out_h, wg_h), (out_v, wg_v), s_in)
    second = pieces((out_v, wg_v), (out_f, wg_f), s_out)
    for c in first:
        c.start()
    for a, b in zip(first, second):
        a.wait()
        b.start()
    for c in second:
        c.wait()


def body(sheet, w_query, w_key, w_value, cotangent, lengths):
    scale = float((HEAD_DIM * sheet.shape[0] * lax.axis_size("rows")) ** -0.5)
    vmem = pl.BlockSpec(memory_space=pltpu.VMEM)
    anyw = pl.BlockSpec(memory_space=pl.ANY)
    dma = pltpu.SemaphoreType.DMA
    V = pltpu.VMEM
    rows = (3, 1024, 256)
    scratch = [
        V((16, 256, 768), BF16), V((576, 768), BF16), V((768, 384), BF16), V((768, 192), BF16), V((16, 256), F32),
        V(rows, BF16), V(rows, BF16), V(rows, BF16), V(rows, BF16),
        V((3, 2, 4, 48, 768), BF16), V((3, 4, 48, 192), BF16), V((4, 192, 576), BF16),
        V((3,) + rows, BF16), V((3,) + rows, BF16), V((3,) + rows, BF16),
        V((2, 2, 3, 256, 128), F32), V((2, 3, 256, 128), F32), V((2, 3, 256, 128), F32),
        V((2, 3, 3, 64, 128), F32), V((2, 3, 64, 128), F32),
        V((2, 7, 3, 8, 128), F32), V((2, 2, 3, 8, 128), F32),
        V((2, 32, 3, 16, 128), BF16), V((3, 2, 32, 3, 16, 128), BF16),
        V((3, 256, 256), BF16), V((3, 256, 256), BF16),
        V((4, 192, 1024), F32), V((16, 192, 256), BF16),
        V((576, 768), F32), V((768, 576), F32), V((2, 8, 48, 576), BF16), V((8, 48, 576), BF16),
        V((7, 48, 576), BF16), V((56, 576), F32), V((4, 16, 576), BF16), V((3, 16, 576), BF16),
        dma((4,)), dma((1,)), dma((1,)), dma((1,)),
    ]
    shapes = [
        (2, 2), (2, 2), (2, 2), (1, 1), (1, 1), (1, 3), (1, 1),
        (2, 2), (4, 4), (2, 2), (2, (2, 8)), (2, 4), (1, 1), (1, 1), (1, 3), (1, 3),
        (1, 1), (1, 1), (1, 1),
    ]
    for out_shape, in_shape in shapes:
        scratch += [dma(shape if isinstance(shape, tuple) else (shape,)) for shape in (out_shape, in_shape)]
    out, wg = pl.pallas_call(
        functools.partial(kernel, scale),
        out_shape=(jax.ShapeDtypeStruct((16, 192, 256), BF16), jax.ShapeDtypeStruct((12, 3, 192), F32)),
        in_specs=[anyw] * 5 + [pl.BlockSpec(memory_space=pltpu.SMEM)],
        out_specs=(anyw, vmem),
        scratch_shapes=scratch,
        compiler_params=pltpu.CompilerParams(
            collective_id=0, has_side_effects=True, vmem_limit_bytes=62 * 1024 * 1024
        ),
    )(
        sheet, w_query.T, w_key.T, w_value.T,
        cotangent.transpose(0, 2, 1).reshape(16, NH, HEAD_DIM, 256), lengths,
    )
    out, wg = pl.pallas_call(
        place,
        out_shape=(jax.ShapeDtypeStruct(out.shape, BF16), jax.ShapeDtypeStruct(wg.shape, F32)),
        in_specs=[anyw, anyw],
        out_specs=(anyw, anyw),
        scratch_shapes=[V(out.shape, BF16), V(wg.shape, F32), dma((5,)), dma((5,))],
    )(out, wg)
    return out.transpose(0, 2, 1), wg


def solution(mesh):
    in_specs = (
        P("rows", None, None),
        P(None, "heads"),
        P(None, "heads"),
        P(None, "heads"),
        P("rows", None, "heads"),
        P("rows"),
    )
    out_specs = (P("rows", None, "heads"), P("rows", None, "heads"))
    return jax.shard_map(body, mesh=mesh, in_specs=in_specs, out_specs=out_specs, check_vma=False)
```

time: 96.8 us -> 78.8 us (0.81)
  Pallas kernels: 92.8 us -> 78 us
  local copies, waits for them, and re-layouts: 3.33 us -> 0 us
    pallas_call x1, Pallas kernels: 92.8 us -> 75.8 us  [body(): pl.pallas_call(functools.partial(kernel, scale), out_shape=(jax.ShapeDtyp...]
    unnamed x4 -> x0, local copies, waits for them, and re-layouts: 3.33 us -> none
    pallas_call x0 -> x1, Pallas kernels: none -> 2.25 us  [body(): pl.pallas_call(place, out_shape=(jax.ShapeDtypeStruct(out.shape, BF16), j...]
where the time goes in v4:
time: 78.8 us; the launch traced here: 78.6 us
  Pallas kernels  78 us (99%)
    pallas_call x1, Pallas kernels, body(): pl.pallas_call(functools.partial(kernel, scale), out_shape=(jax.ShapeDtyp...  75.8 us
    pallas_call x1, Pallas kernels, body(): pl.pallas_call(place, out_shape=(jax.ShapeDtypeStruct(out.shape, BF16), j...  2.25 us

profile of v4, /device:TPU:1, one launch (start us, length us, event | category | flops | bytes accessed | tf_op | source)
XLA Modules:
  0.0 78.6 jit_solution(9017133798334705835)
XLA Ops:
  0.6 75.8 %shard_map.77 = (bf16[16,192,256]{2,1,0:T(8,128)(2,1)}, f32[12,3,192]{2,1,0:T(4,128)}) custom-call(bf16[16,256,768]{2,1,0:T(8,128)(2,1)} %sheet_h.1, bf16[192,768]{1,0:T(8,128)(2,1)} %bitcast.8, bf16[192,768]{1,0:T(8,128)(2,1)} %bitcast.9, bf16[192,768]{1,0:T(8,128)(2,1)} %bitcast.10, bf16[16,3,64,256]{3,2,1,0:T(8,128)(2,1)} %bitcast.7, s32[16]{0:T(128)} %lens.1), custom_call_target="tpu_custom_call" | custom-call | tf_op jit(solution)/shard_map/pallas_call | solution.py:578
  76.4 2.2 %shard_map.78 = (bf16[16,192,256]{2,1,0:T(8,128)(2,1)}, f32[12,3,192]{2,1,0:T(4,128)}) custom-call(bf16[16,192,256]{2,1,0:T(8,128)(2,1)} %get-tuple-element.6.out_h, f32[12,3,192]{2,1,0:T(4,128)} %get-tuple-element.7.wg_h), custom_call_target="tpu_custom_call" | custom-call | tf_op jit(solution)/shard_map/pallas_call | solution.py:591

commit v5 on v4

--- a/solution.py
+++ b/solution.py
@@ -88,8 +88,7 @@
 
     for t in range(3):
         w_copy(t).start()
-    for i in range(4):
-        sheet_copy(i).start()
+    sheet_copy(0).start()
 
     barrier = pltpu.get_barrier_semaphore()
     peers = [partner] + ypeer + xpeer + zpeer
@@ -112,6 +111,8 @@
         return 0
 
     pltpu.make_async_copy(w_t, w_t, s_w.at[0]).wait()
+    for i in range(1, 4):
+        sheet_copy(i).start()
     for r in range(16):
         cot_copy(r).start()
     w_vc[...] = w_t[384:576].T
@@ -258,17 +259,16 @@
     sent(wv_far.at[:, 0], swy.at[1])
     lax.fori_loop(2, 4, value_rows, 0)
     pltpu.make_async_copy(g_t, g_t, s_cot.at[0]).wait()
-    near([0, 1, 2])
     outer(0, g_t, v_t)
     query_rows(q_t, k_t, own_weights, 0, 1)
     add_core(0)
     query_rows(q_t, k_t, own_weights, 1, 4)
     outer(1, q_t, k_t)
-    near([3])
-    add_core(1)
     arrived(w_far.at[:, 0, 0], rwy.at[0])
     arrived(wv_far.at[:, 0], rwy.at[1])
     send(wz_copies())
+    near([0, 1, 2])
+    add_core(1)
     send(wx_copies())
     sent(w_far.at[:, 0, 0], sww.at[0])
     sent(wv_far.at[:, 0], sww.at[1])
@@ -279,8 +279,8 @@
     w_c[...] = w_t[0:384].T
     w_out[0, :, 0:384] = w_c[rows_y, :]
     w_out[0, :, 384:576] = w_vc[rows_y, :]
+    add_x(1)
     relay([0])
-    add_x(1)
     arrived(w_far.at[:, 0, 0], rww.at[0])
     arrived(wv_far.at[:, 0], rww.at[1])
     wc_copy = remote(w_far.at[0, core], w_far.at[0, core], swc.at[0], rwc.at[0], partner)
@@ -289,6 +289,7 @@
     sent(w_far.at[0, 0], swc.at[0])
     wc_copy.wait_recv()
     far_rows(0)
+    relay([1])
     add_z(0)
     add_z(1)
 
@@ -316,7 +317,7 @@
     send(ty)
     sent(gat.at[0, 0:7], sgz.at[0])
     sent(gat_far.at[:, 0, 0], sty.at[0])
-    near([4, 5, 6, 7])
+    near([3, 4, 5, 6, 7])
 
     xblock = pl.ds(pl.multiple_of(x * NZ, NZ), NZ)
 
@@ -347,15 +348,15 @@
     arrived(wv_far.at[:, 0:2], rww.at[3])
     send([wd_copy])
     sent(w_far.at[1:3, 0], swc.at[1])
+    wd_copy.wait_recv()
+    far_rows(1)
     arrived(gat.at[0, 0:7], rgz.at[0])
     send([gx_copy(k) for k in range(NX - 1)])
     send([gc_copy(0)])
     arrived(gat_far.at[:, 0, 0], rty.at[0])
     send([oz_copy(k) for k in range(NZ - 1)])
-    wd_copy.wait_recv()
-    far_rows(1)
     far_rows(2)
-    relay([1, 2])
+    relay([2])
     for k in range(NX - 1):
         gx_copy(k).wait_recv()
         send([gc_copy(k + 1)])
@@ -445,13 +446,6 @@
         arrived(gat_far.at[s, 0], roc.at[s])
         unpack(lambda ch, h: gat_far[s, ch, :, h])
         back_qk(q_far.at[s], k_far.at[s])
-
-    def far_qk_out(s):
-        def one(c, _):
-            acc[c] += nn(w_out[s + 1, :, 0:384], gathered((q_far.at[s], k_far.at[s]), c))
-            return 0
-
-        lax.fori_loop(0, 4, one, 0)
 
     def far_v(s, h, c):
         at = pl.multiple_of(c * 256, 256)
@@ -500,7 +494,6 @@
     send([wx_copy(k) for k in range(NX - 1)])
     sent(wx_recv, swx.at[0])
 
-    far_qk_out(1)
 
     def out_copy(c):
         rows = pl.ds(4 * c, 4)
@@ -508,7 +501,8 @@
 
     for c in range(4):
         arrived(g_far.at[1, :, 256 * c:256 * c + 256, :], rgr.at[c])
-        tot = acc[c] + nn(w_out[2, :, 384:576], far_v_mat(1, c))
+        grads = jnp.concatenate([gathered((q_far.at[1], k_far.at[1]), c), far_v_mat(1, c)], axis=0)
+        tot = acc[c] + nn(w_out[2], grads)
         for n in range(4):
             out_v[4 * c + n] = tot[:, 256 * n:256 * n + 256].astype(BF16)
         out_copy(c).start()

time: 78.8 us -> 77.3 us (0.981)
  Pallas kernels: 78 us -> 76.5 us
    pallas_call x1, Pallas kernels: 75.8 us -> 74.3 us  [body(): pl.pallas_call(functools.partial(kernel, scale), out_shape=(jax.ShapeDtyp...]
where the time goes in v5:
time: 77.3 us; the launch traced here: 77.2 us
  Pallas kernels  76.5 us (99%)
    pallas_call x1, Pallas kernels, body(): pl.pallas_call(functools.partial(kernel, scale), out_shape=(jax.ShapeDtyp...  74.3 us
    pallas_call x1, Pallas kernels, body(): pl.pallas_call(place, out_shape=(jax.ShapeDtypeStruct(out.shape, BF16), j...  2.25 us

profile of v5, /device:TPU:1, one launch (start us, length us, event | category | flops | bytes accessed | tf_op | source)
XLA Modules:
  0.0 77.2 jit_solution(13004339334772048422)
XLA Ops:
  0.6 74.3 %shard_map.77 = (bf16[16,192,256]{2,1,0:T(8,128)(2,1)}, f32[12,3,192]{2,1,0:T(4,128)}) custom-call(bf16[16,256,768]{2,1,0:T(8,128)(2,1)} %sheet_h.1, bf16[192,768]{1,0:T(8,128)(2,1)} %bitcast.8, bf16[192,768]{1,0:T(8,128)(2,1)} %bitcast.9, bf16[192,768]{1,0:T(8,128)(2,1)} %bitcast.10, bf16[16,3,64,256]{3,2,1,0:T(8,128)(2,1)} %bitcast.7, s32[16]{0:T(128)} %lens.1), custom_call_target="tpu_custom_call" | custom-call | tf_op jit(solution)/shard_map/pallas_call | solution.py:572
  74.9 2.2 %shard_map.78 = (bf16[16,192,256]{2,1,0:T(8,128)(2,1)}, f32[12,3,192]{2,1,0:T(4,128)}) custom-call(bf16[16,192,256]{2,1,0:T(8,128)(2,1)} %get-tuple-element.6.out_h, f32[12,3,192]{2,1,0:T(4,128)} %get-tuple-element.7.wg_h), custom_call_target="tpu_custom_call" | custom-call | tf_op jit(solution)/shard_map/pallas_call | solution.py:585

commit v6 on v5

--- a/solution.py
+++ b/solution.py
@@ -250,9 +250,10 @@
         w_out[s + 1, :, 0:384] = w_c[rows_y, :]
         w_out[s + 1, :, 384:576] = wv_far[s].reshape(192, 192)
 
-    def far_rows(s):
-        far_weights(s)
-        query_rows(q_far.at[s], k_far.at[s], lambda: w_far[s].reshape(384, 768), 0, 4)
+    def far_rows(s, lo, hi):
+        if lo == 0:
+            far_weights(s)
+        query_rows(q_far.at[s], k_far.at[s], lambda: w_far[s].reshape(384, 768), lo, hi)
 
     send(wy_copies())
     sent(w_far.at[:, 0, 0], swy.at[0])
@@ -288,7 +289,7 @@
     send([wc_copy])
     sent(w_far.at[0, 0], swc.at[0])
     wc_copy.wait_recv()
-    far_rows(0)
+    far_rows(0, 0, 4)
     relay([1])
     add_z(0)
     add_z(1)
@@ -349,13 +350,14 @@
     send([wd_copy])
     sent(w_far.at[1:3, 0], swc.at[1])
     wd_copy.wait_recv()
-    far_rows(1)
+    far_rows(1, 0, 2)
     arrived(gat.at[0, 0:7], rgz.at[0])
     send([gx_copy(k) for k in range(NX - 1)])
     send([gc_copy(0)])
     arrived(gat_far.at[:, 0, 0], rty.at[0])
     send([oz_copy(k) for k in range(NZ - 1)])
-    far_rows(2)
+    far_rows(1, 2, 4)
+    far_rows(2, 0, 4)
     relay([2])
     for k in range(NX - 1):
         gx_copy(k).wait_recv()
@@ -403,24 +405,25 @@
         return 0
 
     lax.fori_loop(0, NH, back_v, 0)
+    relay([3])
+    wg_acc[...] = jnp.zeros_like(wg_acc)
+
+    def own_wg(c, _):
+        wg_acc[...] += nn(gathered((q_t, k_t, v_t), c), sheet[pl.ds(4 * c, 4)].reshape(1024, 768))
+        return 0
+
+    def own_out(c, _):
+        acc[c] = nn(w_out[0], gathered((q_t, k_t, v_t), c))
+        return 0
+
+    lax.fori_loop(0, 1, own_wg, 0)
     arrived(gat_far.at[:, 0, 0:7], roz.at[0])
     sent(gat_far.at[:, 0, 0:7], soz.at[0])
     send([ox_copy(s, k) for s in (0, 2, 1) for k in range(NX - 1)])
     send([oc_copy(s, 0) for s in range(NY - 1)])
     sent(gat_far.at[:, 0, 0:24], sox.at[0])
     sent(gat_far.at[:, 0], soc.at[0])
-    relay([3])
-    wg_acc[...] = jnp.zeros_like(wg_acc)
-
-    def own_wg(c, _):
-        wg_acc[...] += nn(gathered((q_t, k_t, v_t), c), sheet[pl.ds(4 * c, 4)].reshape(1024, 768))
-        return 0
-
-    def own_out(c, _):
-        acc[c] = nn(w_out[0], gathered((q_t, k_t, v_t), c))
-        return 0
-
-    lax.fori_loop(0, 4, own_wg, 0)
+    lax.fori_loop(1, 4, own_wg, 0)
     wg_n[...] = wg_acc[...].T
     for gc in range(2):
         for gz_ in range(NZ):

time: 77.3 us -> 77.3 us (level)
  no operation moved by 1% of the time
where the time goes in v6:
time: 77.3 us; the launch traced here: 77.2 us
  Pallas kernels  76.5 us (99%)
    pallas_call x1, Pallas kernels, body(): pl.pallas_call(functools.partial(kernel, scale), out_shape=(jax.ShapeDtyp...  74.3 us
    pallas_call x1, Pallas kernels, body(): pl.pallas_call(place, out_shape=(jax.ShapeDtypeStruct(out.shape, BF16), j...  2.25 us

profile of v6, /device:TPU:1, one launch (start us, length us, event | category | flops | bytes accessed | tf_op | source)
XLA Modules:
  0.0 77.2 jit_solution(9684746492226122455)
XLA Ops:
  0.6 74.3 %shard_map.77 = (bf16[16,192,256]{2,1,0:T(8,128)(2,1)}, f32[12,3,192]{2,1,0:T(4,128)}) custom-call(bf16[16,256,768]{2,1,0:T(8,128)(2,1)} %sheet_h.1, bf16[192,768]{1,0:T(8,128)(2,1)} %bitcast.8, bf16[192,768]{1,0:T(8,128)(2,1)} %bitcast.9, bf16[192,768]{1,0:T(8,128)(2,1)} %bitcast.10, bf16[16,3,64,256]{3,2,1,0:T(8,128)(2,1)} %bitcast.7, s32[16]{0:T(128)} %lens.1), custom_call_target="tpu_custom_call" | custom-call | tf_op jit(solution)/shard_map/pallas_call | solution.py:575
  74.9 2.2 %shard_map.78 = (bf16[16,192,256]{2,1,0:T(8,128)(2,1)}, f32[12,3,192]{2,1,0:T(4,128)}) custom-call(bf16[16,192,256]{2,1,0:T(8,128)(2,1)} %get-tuple-element.6.out_h, f32[12,3,192]{2,1,0:T(4,128)} %get-tuple-element.7.wg_h), custom_call_target="tpu_custom_call" | custom-call | tf_op jit(solution)/shard_map/pallas_call | solution.py:588
